TPU v7x, 512 devices: a whole 4x4x16 slice. The times are simulated.
512 devices in a mesh: seq: 32 (over z, core), hid: 16 (over x, y).
Axes of the slice: x: 4, y: 4, z: 16, core: 2. Of those that a mesh axis runs over, the one named last changes fastest.
Arguments:
- activations: bfloat16 [16384, 4096], P('seq'), may hold values from -6 to 6
- w_inner: bfloat16 [4096, 4096], P('seq', 'hid'), may hold values from -0.09375 to 0.09375
- w_gate: bfloat16 [4096, 4096], P('seq', 'hid'), may hold values from -0.09375 to 0.09375
- w_groups: bfloat16 [4096, 1024], P('seq'), may hold values from -0.09375 to 0.09375
- w_step: bfloat16 [4096, 64], P('seq'), may hold values from -0.09375 to 0.09375
- w_out: bfloat16 [4096, 4096], P('seq', 'hid'), may hold values from -0.09375 to 0.09375
- conv_inner: float32 [4, 4096], P(None, 'hid'), may hold values from -3 to 3
- conv_groups: float32 [4, 1024], replicated, may hold values from -3 to 3
- step_bias: float32 [64], P('hid'), may hold values from -4 to 0
- decay_log: float32 [64], P('hid'), may hold values from -9 to -1
- skip_gain: float32 [64], P('hid'), may hold values from 0.5 to 1.5
- norm_gain: float32 [4096], P('hid'), may hold values from 0.5 to 1.5
Outputs:
- layer_out: bfloat16 [16384, 4096], P('seq', 'hid')
All inputs are finite; a program needn't handle non-finite values.
Results may differ from a plain program's by a relative error of at most 0.02.
Values may be sent and summed in bfloat16 or wider, within the bound.
A program may use at most 64 MiB of HBM per device.

v0:
```python
import jax
import jax.numpy as jnp
from jax import lax
from jax.sharding import PartitionSpec as P

HEADS = 64
P_SIZE = 64
N = 128
G = 4
Q = 256
K = 4
INNER = 4096


def from_behind(block, axis, distance):
    devices = range(lax.axis_size(axis))
    route = [(i - distance, i) for i in devices if i - distance in devices]
    return lax.ppermute(block, axis, route)


def carried_in(array, axis, join, neutral):
    place = lax.axis_index(axis)
    gathered = jax.tree.map(
        lambda a, kind: lax.all_gather(a.astype(kind), axis), array, (jnp.bfloat16, jnp.bfloat16)
    )
    state = jax.tree.map(lambda a, e: jnp.zeros_like(a) + jnp.asarray(e, a.dtype), array, neutral)

    def one(step, state):
        return join(
            state,
            jax.tree.map(
                lambda a, own: lax.dynamic_index_in_dim(a, step, 0, False).astype(own.dtype),
                gathered,
                array,
            ),
        )

    return lax.fori_loop(0, place, one, state)


def causal_conv(values, before, kernel):
    length = values.shape[0]
    extended = jnp.concatenate([before, values], axis=0)
    summed = jnp.zeros(values.shape, jnp.float32)
    for position in range(kernel.shape[0]):
        summed = (
            summed + extended[position : position + length].astype(jnp.float32) * kernel[position]
        )
    return jax.nn.silu(summed).astype(jnp.bfloat16)


def combine_states(earlier, later):
    return (earlier[0] * later[0], later[0][:, None, None] * earlier[1] + later[1])


def roll_state(state, inputs):
    total_here, fresh_here = inputs
    return (jnp.exp(total_here)[:, None, None] * state + fresh_here, state)


def local(
    activations,
    w_inner,
    w_gate,
    w_groups,
    w_step,
    w_out,
    conv_inner,
    conv_groups,
    step_bias,
    decay_log,
    skip_gain,
    norm_gain,
):
    tok_rows = activations.shape[0]
    heads_dev = step_bias.shape[0]
    width_dev = w_inner.shape[1]
    head_block = lax.axis_index("hid")
    group_cols = 2 * N
    group_index = head_block * heads_dev // (HEADS // G)
    step_cols = lax.dynamic_slice_in_dim(w_step, head_block * heads_dev, heads_dev, 1)
    own_cols = lax.dynamic_slice_in_dim(w_groups, group_index * group_cols, group_cols, 1)
    piece_inner = lax.all_gather(w_inner, "seq", axis=0, tiled=True)
    piece_gate = lax.all_gather(w_gate, "seq", axis=0, tiled=True)
    piece_groups = lax.all_gather(own_cols, "seq", axis=0, tiled=True)
    piece_step = lax.all_gather(step_cols, "seq", axis=0, tiled=True)
    piece_out = lax.all_gather(w_out, "seq", axis=0, tiled=True)
    acc_inner = jnp.dot(activations, piece_inner, preferred_element_type=jnp.float32)
    acc_gate = jnp.dot(activations, piece_gate, preferred_element_type=jnp.float32)
    acc_groups = jnp.dot(activations, piece_groups, preferred_element_type=jnp.float32)
    acc_step = jnp.dot(activations, piece_step, preferred_element_type=jnp.float32)
    groups_in = acc_groups.astype(jnp.bfloat16)
    inner_in = acc_inner.astype(jnp.bfloat16)
    gate_in = acc_gate.astype(jnp.bfloat16)
    conv_group = lax.dynamic_slice_in_dim(conv_groups, group_index * group_cols, group_cols, 1)
    tail_rows = K - 1
    inner_prev, groups_prev = from_behind(
        (inner_in[tok_rows - tail_rows :], groups_in[tok_rows - tail_rows :]), "seq", 1
    )
    inner_conv = causal_conv(inner_in, inner_prev, conv_inner)
    groups_conv = causal_conv(groups_in, groups_prev, conv_group)
    step_size = jax.nn.softplus(acc_step + step_bias)
    rates = -jnp.exp(decay_log)
    span_count = tok_rows // Q
    heads_x = inner_conv.reshape(span_count, Q, heads_dev, P_SIZE)
    b_in = groups_conv[:, :N].reshape(span_count, Q, N)
    c_out = groups_conv[:, N:].reshape(span_count, Q, N)
    block_dt = step_size.reshape(span_count, Q, heads_dev)
    cum_decay = jnp.cumsum(block_dt * rates, axis=1)
    scores = jnp.einsum("ctn,csn->cts", c_out, b_in, preferred_element_type=jnp.float32)
    ahead = jnp.arange(Q)[:, None] >= jnp.arange(Q)[None, :]
    decay_t = jnp.swapaxes(cum_decay, 1, 2)
    gap = jnp.where(ahead, decay_t[:, :, :, None] - decay_t[:, :, None, :], -1e30)
    mixing = (scores[:, None] * jnp.exp(gap) * jnp.swapaxes(block_dt, 1, 2)[:, :, None, :]).astype(
        jnp.bfloat16
    )
    intra = jnp.einsum("chts,cshp->cthp", mixing, heads_x, preferred_element_type=jnp.float32)
    span_total = cum_decay[:, -1]
    weights_in = jnp.exp(span_total[:, None, :] - cum_decay) * block_dt
    weighted = (b_in[:, :, None, :] * weights_in[:, :, :, None]).astype(jnp.bfloat16)
    fresh = jnp.einsum("cshn,cshp->chnp", weighted, heads_x, preferred_element_type=jnp.float32)
    zero_state = jnp.zeros((heads_dev, N, P_SIZE), jnp.float32)
    local_end, starts = lax.scan(roll_state, zero_state, (span_total, fresh))
    log_total = jnp.sum(span_total, axis=0)
    prior = jnp.cumsum(span_total, axis=0) - span_total
    identity = (jnp.ones((heads_dev,), jnp.float32), zero_state)
    state_in = carried_in((jnp.exp(log_total), local_end), "seq", combine_states, identity)[1]
    span_in = starts + jnp.exp(prior)[:, :, None, None] * state_in[None]
    inter = jnp.einsum(
        "ctn,chnp->cthp", c_out.astype(jnp.float32), span_in, precision=lax.Precision.HIGHEST
    )
    inter = inter * jnp.exp(cum_decay)[:, :, :, None]
    mixed = (intra + inter).reshape(tok_rows, width_dev) + jnp.repeat(
        skip_gain, P_SIZE
    ) * inner_conv.astype(jnp.float32)
    gated = mixed * jax.nn.silu(gate_in.astype(jnp.float32))
    squares = lax.psum(jnp.sum(gated * gated, axis=1), "hid")
    normed = (gated * lax.rsqrt(squares / INNER + 1e-05)[:, None] * norm_gain).astype(jnp.bfloat16)
    terms = lax.dot_general(
        normed, piece_out, (((1,), (1,)), ((), ())), preferred_element_type=jnp.float32
    )
    return lax.psum_scatter(terms.astype(jnp.bfloat16), "hid", scatter_dimension=1, tiled=True)


def solution(mesh):
    in_specs = (
        P("seq", None),
        P("seq", "hid"),
        P("seq", "hid"),
        P("seq", None),
        P("seq", None),
        P("seq", "hid"),
        P(None, "hid"),
        P(),
        P("hid"),
        P("hid"),
        P("hid"),
        P("hid"),
    )
    out_specs = P("seq", "hid")
    return jax.shard_map(local, mesh=mesh, in_specs=in_specs, out_specs=out_specs, check_vma=False)
```

profile of v0, /device:TPU:1, one launch (start us, length us, event | category | flops | bytes accessed | tf_op | source)
XLA Modules:
  0.0 480.2 jit_solution(4946631433308588536)
XLA Ops:
  6.5 0.9 copy-done
  7.5 0.6 constant_dynamic-slice_fusion.4
  8.1 0.0 all-gather.10.cloned.1.call-update
  8.1 0.0 all-gather.8.cloned.1.call-start
  8.2 0.7 all-gather.8.cloned.1.call-update
  8.9 0.0 all-gather.16.cloned.1.call-start
  9.0 0.7 constant_dynamic-slice_fusion.3
  9.7 37.6 %all_gather.27 = bf16[4096,4]{0,1:T(4,128)(2,1)S(1)} all-gather(bf16[128,4]{0,1:T(4,128)(2,1)S(1)} %constant_dynamic-slice_fusion.3), channel_id=1, replica_groups=mesh['seq'=32,'hid'=16] {'seq'}, dimensions={0}, use_global_device_ids=true | all-gather | bytes 33792 | tf_op jit(solution)/shard_map/all_gather | solution.py:86
  47.3 0.7 exponential_negate_fusion
  48.0 3.4 compare_select_fusion
  51.4 0.1 multiply_bitcast_fusion
  51.5 2.4 reduce-window.6
  53.9 0.1 slice.96
  54.0 0.1 copy.79
  54.1 0.1 copy.80
  54.2 0.1 broadcast_add_fusion
  54.3 0.9 constant_dynamic-slice_fusion.2
  55.3 0.2 slice_reduce_fusion
  55.5 0.1 bitcast_exponential_fusion
  55.5 31.2 %all-gather.10.cloned.1.call-done = bf16[4096,256]{1,0:T(8,128)(2,1)} async-done(((bf16[128,256]{1,0:T(8,128)(2,1)}), bf16[4096,256]{1,0:T(8,128)(2,1)}) %all-gather.10.cloned.1.call-update) | async-done | bytes 2097168 | tf_op jit(solution)/shard_map/all_gather | solution.py:85
  86.7 4.1 fusion.4
  90.8 3.2 collective-permute-start.1
  94.1 63.1 %all-gather.8.cloned.1.call-done = bf16[4096,256]{1,0:T(8,128)(2,1)} async-done(((bf16[128,256]{1,0:T(8,128)(2,1)}), bf16[4096,256]{1,0:T(8,128)(2,1)}) %all-gather.8.cloned.1.call-update) | async-done | bytes 2097168 | tf_op jit(solution)/shard_map/all_gather | solution.py:83
  157.2 4.1 convolution_convert_fusion.3
  161.3 3.3 collective-permute-start
  164.7 0.3 multiply_convert_fusion.5
  165.1 0.3 collective-permute-done
  165.4 0.3 multiply_convert_fusion.6
  165.7 0.2 reshape.122
  166.0 0.3 copy.81
  166.3 0.8 fusion.12
  167.1 0.3 while.26
  167.1 0.1 bitcast_add_fusion.2
  167.3 0.1 bitcast_add_fusion.2
  167.4 0.7 copy.84
  168.2 0.0 all-gather.12.cloned.1.call-start
  168.2 0.5 all-gather.12.cloned.1.call-update
  168.7 0.0 all-gather.14.cloned.1.call-start
  168.8 0.5 all-gather.14.cloned.1.call-update
  169.3 0.0 reduce-scatter.2.cloned.1.call-start
  169.4 1.3 dynamic-slice
  171.4 0.2 dynamic-update-slice
  171.6 46.6 %all-reduce = bf16[128]{0:T(256)(128)(2,1)S(1)} all-reduce(bf16[128]{0:T(256)(128)(2,1)S(1)} %dynamic-update-slice), channel_id=2, replica_groups=mesh['seq'=32,'hid'=16] {'seq'}, use_global_device_ids=true, to_apply=%add | all-reduce | flops 128 | bytes 512
  218.3 0.1 reshape.112
  218.4 0.1 broadcast_in_dim.25
  218.5 0.1 mul.255
  218.6 0.2 fusion.24
  218.8 20.0 %all-gather.16.cloned.1.call-done = bf16[128,128,64]{1,2,0:T(8,128)(2,1)} async-done(((bf16[4,128,64]{1,2,0:T(8,128)(2,1)}), bf16[128,128,64]{1,2,0:T(8,128)(2,1)}) %all-gather.16.cloned.1.call-update) | async-done | bytes 2097168 | tf_op jit(solution)/shard_map/all_gather | solution.py:24
  238.8 1.1 while.25
  238.9 0.9 constant_dynamic-slice_fusion.6
  239.7 0.1 copy.99
  239.9 0.1 convert_add_fusion.2
  240.0 0.1 multiply_add_fusion
  240.1 0.2 copy.86
  240.3 0.4 fusion.25
  240.7 0.8 fusion.2
  241.5 0.4 copy.93
  241.8 0.6 reshape.121
  242.5 66.8 %all-gather.12.cloned.1.call-done = bf16[4096,256]{1,0:T(8,128)(2,1)} async-done(((bf16[128,256]{1,0:T(8,128)(2,1)}), bf16[4096,256]{1,0:T(8,128)(2,1)}) %all-gather.12.cloned.1.call-update) | async-done | bytes 2097168 | tf_op jit(solution)/shard_map/all_gather | solution.py:84
  309.3 4.3 multiply_reduce_fusion
  313.6 33.2 %psum.7 = f32[512]{0:T(512)S(1)} all-reduce(f32[512]{0:T(512)S(1)} %get-tuple-element.172), channel_id=1, replica_groups=mesh['seq'=32,'hid'=16] {'hid'}, use_global_device_ids=true, to_apply=%region_9.10 | all-reduce | flops 512 | bytes 4096 | tf_op jit(solution)/shard_map/psum | solution.py:137
  346.8 32.7 %all-gather.14.cloned.1.call-done = bf16[4096,256]{1,0:T(8,128)(2,1)} async-done(((bf16[128,256]{1,0:T(8,128)(2,1)}), bf16[4096,256]{1,0:T(8,128)(2,1)}) %all-gather.14.cloned.1.call-update) | async-done | bytes 2097168 | tf_op jit(solution)/shard_map/all_gather | solution.py:87
  379.5 4.8 %convolution_convert_fusion = bf16[512,4096]{1,0:T(8,128)(2,1)} fusion(bf16[4096,256]{1,0:T(8,128)(2,1)} %all-gather.14.cloned.1.call-done, f32[512,256]{1,0:T(8,128)S(1)} %get-tuple-element.173, f32[256]{0:T(256)S(1)} %copy-done.1, f32[512]{0:T(512)S(1)} %add_rsqrt_fusion), kind=kOutput, calls=%fused_computation.8 | convolution fusion | flops 1076232192 | bytes 6818816 | tf_op jit(solution)/shard_map/dot_general | solution.py:139
  384.4 88.9 %reduce-scatter.2.cloned.1.call-done = bf16[512,256]{1,0:T(8,128)(2,1)} async-done(((bf16[512,4096]{1,0:T(8,128)(2,1)}), bf16[512,256]{1,0:T(8,128)(2,1)}) %reduce-scatter.2.cloned.1.call-update) | async-done | bytes 262160 | tf_op jit(solution)/shard_map/reduce_scatter | solution.py:142
  (34 shorter events, 0.4 us)
Async XLA Ops:
  6.5 1.0 copy-start
  6.5 80.2 %all-gather.10.cloned.1.call-start = ((), (), s32[]{:S(2)}) async-start(), calls=%async_computation.2 | async-start | bytes 2162688 | tf_op jit(solution)/shard_map/all_gather | solution.py:85
  8.1 149.1 %all-gather.8.cloned.1.call-start = ((), (), s32[]{:S(2)}) async-start(), calls=%async_computation.1 | async-start | bytes 2162688 | tf_op jit(solution)/shard_map/all_gather | solution.py:83
  8.9 229.9 %all-gather.16.cloned.1.call-start = ((), (), s32[]{:S(2)}) async-start(), calls=%async_computation.6 | async-start | bytes 2162688 | tf_op jit(solution)/shard_map/all_gather | solution.py:24
  48.0 7.5 %copy-start.2 = (f32[4,256]{1,0:T(4,128)S(1)}, f32[4,256]{1,0:T(4,128)}, u32[]{:S(2)}) copy-start(f32[4,256]{1,0:T(4,128)} %param.22) | copy-start | bytes 12292
  90.8 73.8 %collective-permute-start.1 = (bf16[3,256]{1,0:T(4,128)(2,1)S(1)}, bf16[3,256]{1,0:T(4,128)(2,1)S(1)}, u32[]{:S(2)}, u32[]{:S(2)}) collective-permute-start(bf16[3,256]{1,0:T(4,128)(2,1)S(1)} %slice.89), channel_id=1, source_target_pairs={{0,16},{16,32},{32,48},{48,64},{64,80},{80,96},{96,112},{112,128},... | collective-permute-start | bytes 4616 | tf_op jit(solution)/shard_map/ppermute | solution.py:18
  161.3 4.1 collective-permute-start
  167.1 51.3 %copy-start.3 = (f32[4]{0:T(128)S(1)}, f32[4]{0:T(128)}, u32[]{:S(2)}) copy-start(f32[4]{0:T(128)} %param.26) | copy-start | bytes 52
  168.2 141.2 %all-gather.12.cloned.1.call-start = ((), (), s32[]{:S(2)}) async-start(), calls=%async_computation.3 | async-start | bytes 2162688 | tf_op jit(solution)/shard_map/all_gather | solution.py:84
  168.7 210.8 %all-gather.14.cloned.1.call-start = ((), (), s32[]{:S(2)}) async-start(), calls=%async_computation.4 | async-start | bytes 2162688 | tf_op jit(solution)/shard_map/all_gather | solution.py:87
  169.3 304.0 %reduce-scatter.2.cloned.1.call-start = ((), (), s32[]{:S(2)}) async-start(), calls=%async_computation.5 | async-start | bytes 4456448 | tf_op jit(solution)/shard_map/reduce_scatter | solution.py:142
  242.5 137.1 %copy-start.1 = (f32[256]{0:T(256)S(1)}, f32[256]{0:T(256)}, u32[]{:S(2)}) copy-start(f32[256]{0:T(256)} %param.27) | copy-start | bytes 3076
Sparse Core Ops, SparseCore 0:
  9.5 77.2 all-gather.9
  88.8 68.3 all-gather.7
  168.3 70.5 all-gather.15
  240.8 68.4 all-gather.11
  311.3 68.1 all-gather.13
  384.5 88.7 reduce-scatter.1
where the time goes:
time: 483 us; the launch traced here: 480 us
  waiting for transfers between devices  305 us (63%)
  blocking collectives  118 us (24%)
  matrix products  22.9 us (5%)
  between operations  14.4 us (3%)
  local copies, waits for them, and re-layouts  8.84 us (2%)
  starting transfers between devices  6.77 us (1%)
  other arithmetic  4.83 us (1%)
    reduce_scatter x1, waiting for transfers between devices, local(): lax.psum_scatter(terms.astype(jnp.bfloat16), 'hid', scatter_dimension=1,...  88.9 us
    all_gather x1, waiting for transfers between devices, local(): piece_gate = lax.all_gather(w_gate, 'seq', axis=0, tiled=True)  66.8 us
    all_gather x1, waiting for transfers between devices, local(): piece_inner = lax.all_gather(w_inner, 'seq', axis=0, tiled=True)  63.1 us
    unnamed x1, blocking collectives  46.6 us
    all_gather x1, blocking collectives, local(): piece_step = lax.all_gather(step_cols, 'seq', axis=0, tiled=True)  37.6 us
    psum x1, blocking collectives, local(): squares = lax.psum(jnp.sum(gated * gated, axis=1), 'hid')  33.2 us
    all_gather x1, waiting for transfers between devices, local(): piece_out = lax.all_gather(w_out, 'seq', axis=0, tiled=True)  32.7 us
    all_gather x1, waiting for transfers between devices, local(): piece_groups = lax.all_gather(own_cols, 'seq', axis=0, tiled=True)  31.2 us
  transfers between devices with their start and end apart: 8, of which 7 were waited for; matrix products, arithmetic and copies ran while one was open for 6% of the time, Pallas kernels for 0%

commit v1 on v0

v1 whole, which is shorter than its diff:
```python
import jax
import jax.numpy as jnp
from jax import lax
from jax.experimental import pallas as pl
from jax.experimental.pallas import tpu as pltpu
from jax.sharding import PartitionSpec as P

F32 = jnp.float32
BF16 = jnp.bfloat16
MESH = pl.DeviceIdType.MESH
INNER = 4096
TOK = 512
HALO = 16
NZ = 16
FAR = ((8, 7), (8, 7), (7, 8), (8, 7), (7, 8), (8, 7), (7, 8))


def remote(src, dst, send, recv, device):
    return pltpu.make_async_remote_copy(
        src_ref=src, dst_ref=dst, send_sem=send, recv_sem=recv, device_id=device, device_id_type=MESH
    )


def split(value):
    high = value.astype(BF16)
    return high, (value - high.astype(F32)).astype(BF16)


def kernel(
    act_hbm,
    wi_hbm,
    wg_hbm,
    wo_ref,
    wgr_ref,
    wst_ref,
    tapi_ref,
    tapg_ref,
    bias_ref,
    decay_ref,
    skip_ref,
    gain_ref,
    out_ref,
    act,
    w_in,
    w_gate,
    w_gs,
    land,
    w_out,
    gath,
    acc_i,
    acc_g,
    acc_s,
    bct,
    xc,
    cols,
    e_own,
    e_sib,
    tbuf,
    pbuf,
    psib,
    local_sem,
    halo_sem,
    zs,
    zr,
    bs,
    br,
    a_s,
    a_r,
    a_l,
    ws,
    wr,
    ys,
    yr,
    es,
    ts,
    tr,
    g1s,
    g1r,
    g2s,
    g2r,
):
    s = lax.axis_index("seq")
    h = lax.axis_index("hid")
    z = s // 2
    c = s % 2
    x = h // 4
    y = h % 4

    def dev(zz, cc, hh):
        return {"seq": 2 * zz + cc, "hid": hh}

    def zmod(v):
        return lax.rem(v + 2 * NZ, NZ)

    def hid_at(dx, dy):
        return lax.rem(x + dx + 4, 4) * 4 + lax.rem(y + dy + 4, 4)

    sib = dev(z, 1 - c, h)
    after = {"seq": lax.rem(s + 1, 32), "hid": h}
    extra = {"seq": lax.rem(s + 2 * c - 1 + 32, 32), "hid": h}

    load_act = pltpu.make_async_copy(act_hbm, act.at[pl.ds(HALO, TOK), :], local_sem.at[0])
    own_rows = pl.ds(pl.multiple_of(s * 128, 128), 128)
    load_in = pltpu.make_async_copy(wi_hbm, w_in.at[own_rows, :], local_sem.at[1])
    load_gate = pltpu.make_async_copy(wg_hbm, w_gate.at[own_rows, :], local_sem.at[2])
    load_in.start()
    load_gate.start()
    load_act.start()

    barrier = pltpu.get_barrier_semaphore()
    for step in (1, -1, 2, -2):
        pl.semaphore_signal(barrier, inc=1, device_id=dev(zmod(z + step), c, h), device_id_type=MESH)
    pl.semaphore_signal(barrier, inc=1, device_id=sib, device_id_type=MESH)
    pl.semaphore_signal(barrier, inc=1, device_id=extra, device_id_type=MESH)
    for step in range(1, 16):
        pl.semaphore_signal(
            barrier, inc=1, device_id=dev(z, c, lax.rem(h + step, 16)), device_id_type=MESH
        )

    tile = wgr_ref[:, pl.ds(pl.multiple_of(x * 256 + (y // 2) * 128, 128), 128)].astype(F32).T
    half = jnp.where(y % 2 == 0, tile[:64], tile[64:])
    steps_t = jnp.concatenate([wst_ref[...].astype(F32)] * 2, axis=1).T
    mine = jnp.where(
        x < 2,
        jnp.where(x == 0, steps_t[0:16], steps_t[16:32]),
        jnp.where(x == 2, steps_t[32:48], steps_t[48:64]),
    )
    own_lanes = pl.ds(pl.multiple_of(s * 128, 128), 128)
    w_gs[0:64, own_lanes] = half.astype(BF16)
    w_gs[64:80, own_lanes] = mine.astype(BF16)
    land[z] = (wo_ref[...].astype(F32) * gain_ref[...]).astype(BF16)

    pl.semaphore_wait(barrier, 21)

    send_halo = remote(
        act_hbm.at[pl.ds(TOK - HALO, HALO), :],
        act.at[pl.ds(0, HALO), :],
        halo_sem.at[0],
        halo_sem.at[1],
        after,
    )

    def block(p, zz):
        row = pl.multiple_of((2 * zz + c) * 128, 128)
        if p == 0:
            return w_gs.at[:, pl.ds(row, 128)]
        part = 64 * ((p - 1) % 2)
        if p < 3:
            return w_in.at[pl.ds(row + part, 64), :]
        if p < 5:
            return w_gate.at[pl.ds(row + part, 64), :]
        return land.at[zz, pl.ds(part, 64), :]

    def sib_block(p, zz):
        row = pl.multiple_of((2 * zz + 1 - c) * 128, 128)
        if p == 0:
            return w_gs.at[:, pl.ds(row, 128)]
        part = 64 * ((p - 1) % 2)
        if p < 3:
            return w_in.at[pl.ds(row + part, 64), :]
        return w_gate.at[pl.ds(row + part, 64), :]

    def origin(d, k):
        return zmod(z - k) if d == 0 else zmod(z + k)

    def ring(p, d, k, recv_k):
        ref = block(p, origin(d, k))
        target = zmod(z + 1) if d == 0 else zmod(z - 1)
        return remote(ref, ref, zs.at[p, d, k], zr.at[p, d, recv_k], dev(target, c, h))

    def to_sib(p, d, k):
        ref = block(p, origin(d, k))
        return remote(ref, ref, bs.at[p, d, k], br.at[p, d, k], sib)

    def from_sib(p, d, k):
        ref = sib_block(p, origin(d, k))
        remote(ref, ref, bs.at[p, d, k], br.at[p, d, k], sib).wait_recv()

    def to_owner(p, zz):
        a = p - 5
        dst = w_out.at[
            pl.ds(pl.multiple_of(128 * c, 128) + 64 * a, 64), pl.ds(pl.multiple_of(256 * h, 256), 256)
        ]
        return remote(block(p, zz), dst, a_s.at[a, zz], a_r.at[a, h], dev(z, c, zz)), (
            pltpu.make_async_copy(block(p, zz), dst, a_l.at[a])
        )

    def hand_on(p, d, k):
        if p < 5:
            to_sib(p, d, k).start()
        else:
            zz = origin(d, k)
            far, near = to_owner(p, zz)

            @pl.when(zz != h)
            def _():
                far.start()

            @pl.when(zz == h)
            def _():
                near.start()

    def first(p):
        ring(p, 0, 0, 1).start()
        ring(p, 1, 0, 1).start()
        hand_on(p, 0, 0)

    def event(p, d, k, forward):
        ring(p, d, k, k).wait_recv()
        if forward:
            ring(p, d, k, k + 1).start()
        hand_on(p, d, k)

    def dots(zz):
        col = pl.ds(pl.multiple_of(zz * 256, 256), 256)
        a = act[:, col]
        acc_i[...] += jnp.dot(a, w_in[col, :], preferred_element_type=F32)
        acc_s[...] += lax.dot_general(
            a, w_gs[:, col], (((1,), (1,)), ((), ())), preferred_element_type=F32
        )

    def gate_dots(zz):
        col = pl.ds(pl.multiple_of(zz * 256, 256), 256)
        acc_g[...] += jnp.dot(act[HALO:, col], w_gate[col, :], preferred_element_type=F32)

    first(0)
    load_in.wait()
    first(1)
    first(2)
    send_halo.start()
    load_gate.wait()
    first(3)
    load_act.wait()
    send_halo.wait()
    acc_i[...] = jnp.zeros_like(acc_i)
    acc_s[...] = jnp.zeros_like(acc_s)
    acc_g[...] = jnp.zeros_like(acc_g)

    def lead(k, last):
        for p in (0, 1, 2):
            for d in (0, 1):
                event(p, d, k, k < FAR[p][d] if last else True)

    def behind(k):
        for p in (0, 1, 2):
            for d in (0, 1):
                from_sib(p, d, k)
        dots(origin(0, k))
        dots(origin(1, k))

    lead(1, False)
    for p in (0, 1, 2):
        from_sib(p, 0, 0)
    dots(z)

    def body(k, carry):
        lead(k, False)
        for d in (0, 1):
            event(3, d, k - 1, True)
        behind(k - 1)
        return carry

    lax.fori_loop(2, 7, body, 0)
    lead(7, True)
    for d in (0, 1):
        event(3, d, 6, True)
    first(4)
    behind(6)
    first(5)
    first(6)
    for p in (0, 1, 2):
        event(p, 0 if FAR[p][0] == 8 else 1, 8, False)
    event(3, 0, 7, True)
    event(3, 1, 7, False)
    behind(7)
    for p in (0, 1, 2):
        from_sib(p, 0 if FAR[p][0] == 8 else 1, 8)
    dots(zmod(z + 8))

    def serve(k, last=False):
        for p in (4, 5, 6):
            for d in (0, 1):
                if not last:
                    event(p, d, k, True)
                elif k <= FAR[p][d]:
                    event(p, d, k, k < FAR[p][d])

    def gate_behind(k):
        for p in (3, 4):
            for d in (0, 1):
                from_sib(p, d, k)
        gate_dots(origin(0, k))
        gate_dots(origin(1, k))

    not_first = jnp.where(s == 0, 0.0, 1.0).astype(F32)
    lane128 = lax.broadcasted_iota(jnp.int32, (TOK, 128), 1)
    raw = acc_s[HALO:, :]
    acc_s[...] = acc_s[...].astype(BF16).astype(F32)
    acc_s[0:HALO, :] = acc_s[0:HALO, :] * not_first
    tap_tile = tapg_ref[:, pl.ds(pl.multiple_of(x * 256 + (y // 2) * 128, 128), 128)]
    tap_g = jnp.where(y % 2 == 0, tap_tile, pltpu.roll(tap_tile, 64, axis=1))
    conv = jnp.zeros((TOK, 80), F32)
    for position in range(4):
        conv = conv + acc_s[pl.ds(HALO - 3 + position, TOK), :] * tap_g[position : position + 1, :80]
    conv = conv * jax.nn.sigmoid(conv)
    both = jnp.where(lane128[:, :80] < 64, conv, raw)
    both_t = jnp.concatenate([both, jnp.zeros((TOK, 48), F32)], axis=1).T
    own_cols = pl.ds(pl.multiple_of(64 * y, 64), 64)
    bct[own_cols, :] = both_t[0:64].astype(BF16)

    def y_copy(j, where):
        rows = bct.at[pl.ds(pl.multiple_of(64 * where, 64), 64), :]
        return remote(rows, rows, ys.at[j - 1], yr.at[j - 1], dev(z, c, hid_at(0, j)))

    for j in (1, 3, 2):
        y_copy(j, y).start()

    serve(1)
    event(3, 0, 8, False)

    step4 = jnp.where(
        y < 2,
        jnp.where(y == 0, both_t[64:68], both_t[68:72]),
        jnp.where(y == 2, both_t[72:76], both_t[76:80]),
    )
    step8 = jnp.concatenate([step4, step4], axis=0)
    head = lax.broadcasted_iota(jnp.int32, (8, TOK), 0) % 4
    lane = lax.broadcasted_iota(jnp.int32, (8, TOK), 1)

    def per_head(ref):
        return jnp.where(
            head < 2, jnp.where(head == 0, ref[0], ref[1]), jnp.where(head == 2, ref[2], ref[3])
        )

    v = step8 + per_head(bias_ref)
    dt = jnp.maximum(v, 0.0) + jnp.log1p(jnp.exp(-jnp.abs(v)))
    cum = dt * -jnp.exp(per_head(decay_ref))
    for shift in (1, 2, 4, 8, 16, 32, 64, 128):
        cum = cum + jnp.where(lane % 256 >= shift, pltpu.roll(cum, shift, axis=1), 0.0)
    last = jnp.where(lane < 256, cum[:, 255:256], cum[:, 511:512])
    weight = jnp.exp(last - cum) * dt
    stack = jnp.concatenate([cum, weight, jnp.exp(cum), jnp.zeros((104, TOK), F32)], axis=0)
    cols[...] = stack.T

    def expand(q):
        halves = []
        for i in (0, 2):
            lo = jnp.broadcast_to(cols[:, 8 * q + i : 8 * q + i + 1], (TOK, 128))
            hi = jnp.broadcast_to(cols[:, 8 * q + i + 1 : 8 * q + i + 2], (TOK, 128))
            halves.append(jnp.where(lane128 < 64, lo, hi))
        return jnp.concatenate(halves, axis=1)

    acc_i[...] = acc_i[...].astype(BF16).astype(F32)
    acc_i[0:HALO, :] = acc_i[0:HALO, :] * not_first
    conv = jnp.zeros((TOK, 256), F32)
    for position in range(4):
        conv = conv + acc_i[pl.ds(HALO - 3 + position, TOK), :] * tapi_ref[position : position + 1, :]
    conv = conv * jax.nn.sigmoid(conv)
    xc[...] = conv.astype(BF16)

    serve(2)

    head_lane = lax.broadcasted_iota(jnp.int32, (1, 256), 1) // 64
    weighted = (xc[...].astype(F32) * expand(1)).astype(BF16)
    expcum = expand(2)
    decay0 = expcum[255:256]
    decay1 = expcum[511:512]

    for j in (1, 2, 3):
        y_copy(j, lax.rem(y + 4 - j, 4)).wait()

    fresh0 = jnp.dot(bct[0:128, 0:256], weighted[0:256], preferred_element_type=F32)
    fresh1 = jnp.dot(bct[0:128, 256:512], weighted[256:512], preferred_element_type=F32)
    end_own = decay1 * fresh0 + fresh1
    total_own = decay0 * decay1
    th, tl = split(jnp.broadcast_to(total_own, (8, 256)))
    tail = jnp.concatenate([th.astype(F32), tl.astype(F32)], axis=0).astype(BF16)
    e_own[0:128, :] = end_own.astype(BF16)
    e_own[128:144, :] = tail
    swap = remote(e_own, e_sib, es.at[0], es.at[1], sib)
    swap.start()

    serve(3)
    swap.wait()

    end_sib = e_sib[0:128, :].astype(F32)
    total_sib = e_sib[128:129, :].astype(F32) + e_sib[136:137, :].astype(F32)

    def my_half(value):
        return jnp.where(c == 0, value[:, 0:128], value[:, 128:256])

    second_decay = jnp.where(c == 0, total_sib, total_own)
    chip_end = second_decay * jnp.where(c == 0, end_own, end_sib) + jnp.where(
        c == 0, end_sib, end_own
    )
    chip_total = jnp.broadcast_to(my_half(total_own * total_sib), (8, 128))
    th, tl = split(chip_total)
    tbuf[z, 0:128, :] = my_half(chip_end).astype(BF16)
    tbuf[z, 128:144, :] = jnp.concatenate([th.astype(F32), tl.astype(F32)], axis=0).astype(BF16)

    def t_send(d, k, hop):
        ref = tbuf.at[origin(d, k)]
        target = zmod(z + hop) if d == 0 else zmod(z - hop)
        return remote(ref, ref, ts.at[hop - 1, d, k], tr.at[d, k + hop], dev(target, c, h))

    def t_recv(d, k):
        ref = tbuf.at[origin(d, k)]
        remote(ref, ref, ts.at[0, d, k], tr.at[d, k], sib).wait_recv()

    sent = []

    def t_start(d, k, hop):
        t_send(d, k, hop).start()
        sent.append((d, k, hop))

    for hop in (2, 1):
        for d in (0, 1):
            t_start(d, 0, hop)

    row = lax.broadcasted_iota(jnp.int32, (256, 256), 0)
    column = lax.broadcasted_iota(jnp.int32, (256, 256), 1)
    c_mat = bct[128:256, :].astype(F32).T.astype(BF16)
    intra = []

    def span(q):
        tokens = slice(256 * q, 256 * q + 256)
        scores = jnp.dot(c_mat[tokens], bct[0:128, tokens], preferred_element_type=F32)
        scores = jnp.where(row >= column, scores, 0.0)
        total = jnp.zeros((256, 256), F32)
        for i in range(4):
            gap = jnp.minimum(cols[tokens, i : i + 1] - cum[i : i + 1, tokens], 0.0)
            mixing = (scores * jnp.exp(gap) * dt[i : i + 1, tokens]).astype(BF16)
            x_head = jnp.where(head_lane == i, xc[tokens, :].astype(F32), 0.0).astype(BF16)
            total = total + jnp.dot(mixing, x_head, preferred_element_type=F32)
        return total

    mixed0 = span(0)
    for d in (0, 1):
        t_recv(d, 2)
        for hop in (2, 1):
            t_start(d, 2, hop)
    serve(4)
    mixed1 = span(1)
    skip = jnp.where(
        head_lane < 2,
        jnp.where(head_lane == 0, skip_ref[0], skip_ref[1]),
        jnp.where(head_lane == 2, skip_ref[2], skip_ref[3]),
    )
    xf = xc[...].astype(F32)
    mixed0 = mixed0 + skip * xf[0:256]
    mixed1 = mixed1 + skip * xf[256:512]
    for d in (0, 1):
        t_recv(d, 4)
        for hop in (2, 1):
            t_start(d, 4, hop)
    serve(5)
    for p in (3, 4):
        from_sib(p, 0, 0)
    gate_dots(z)
    for k in (1, 2):
        gate_behind(k)
    t_recv(0, 6)
    for hop in (2, 1):
        t_start(0, 6, hop)
    t_recv(1, 6)
    t_start(1, 6, 1)
    serve(6)
    for k in (3, 4):
        gate_behind(k)
    serve(7, True)
    for k in (5, 6):
        gate_behind(k)
    for d, ks in ((0, (1, 3, 5, 7, 8)), (1, (1, 3, 5, 7))):
        for k in ks:
            t_recv(d, k)

    prefix = jnp.zeros((128, 128), F32)
    for k in range(15, 0, -1):
        zz = zmod(z - k)
        decay = tbuf[zz, 128:129, :].astype(F32) + tbuf[zz, 136:137, :].astype(F32)
        joined = decay * prefix + tbuf[zz, 0:128, :].astype(F32)
        prefix = jnp.where(z >= k, joined, prefix)
    pbuf[...] = prefix
    swap2 = remote(pbuf, psib, es.at[2], es.at[3], sib)
    swap2.start()
    serve(8, True)
    gate_behind(7)
    for p in (3, 4):
        from_sib(p, 0 if FAR[p][0] == 8 else 1, 8)
    gate_dots(zmod(z + 8))
    swap2.wait()
    other = psib[...]
    before = jnp.where(
        c == 0,
        jnp.concatenate([prefix, other], axis=1),
        jnp.concatenate([other, prefix], axis=1),
    )
    state0 = jnp.where(c == 0, before, total_sib * before + end_sib)
    state1 = decay0 * state0 + fresh0

    def gated(q, mixed, state):
        tokens = slice(256 * q, 256 * q + 256)
        high, low = split(state)
        inter = jnp.dot(c_mat[tokens], high, preferred_element_type=F32)
        inter = inter + jnp.dot(c_mat[tokens], low, preferred_element_type=F32)
        mixed = mixed + inter * expcum[tokens]
        gate = acc_g[tokens, :].astype(BF16).astype(F32)
        gath[tokens, pl.ds(pl.multiple_of(256 * h, 256), 256)] = (
            mixed * (gate * jax.nn.sigmoid(gate))
        ).astype(BF16)

    gated(0, mixed0, state0)
    gated(1, mixed1, state1)

    def offset(u, a, b):
        return hid_at(a, b) if u < 2 else hid_at(b, a)

    def part(u, a, b):
        return gath.at[
            pl.ds(128 * u, 128), pl.ds(pl.multiple_of(256 * offset(u, a, b), 256), 256)
        ]

    def g1(u, slot, a):
        ref = part(u, a, 0)
        step = (1, -1, 1 if u % 2 == 0 else -1)[slot]
        return remote(ref, ref, g1s.at[u, slot], g1r.at[u, slot], dev(z, c, offset(u, step, 0)))

    SIDE = (0, -1, 1, 2)

    def g2(u, j, slot, b):
        ref = part(u, SIDE[j], b)
        step = (1, -1, 1 if u % 2 == 0 else -1)[slot]
        return remote(ref, ref, g2s.at[u, j, slot], g2r.at[u, j, slot], dev(z, c, offset(u, 0, step)))

    def g2_start(u, j):
        g2(u, j, 0, 0).start()
        g2(u, j, 1, 0).start()

    units = (0, 2, 1, 3)
    for u in units:
        g1(u, 0, 0).start()
        g1(u, 1, 0).start()
    for u in units:
        g2_start(u, 0)

    def own_out(cc, hh):
        return w_out.at[
            pl.ds(pl.multiple_of(128 * cc, 128), 128), pl.ds(pl.multiple_of(256 * hh, 256), 256)
        ]

    def out_to_sib(hh):
        return remote(own_out(c, hh), own_out(c, hh), ws.at[hh], wr.at[hh], sib)

    def take_out(hh, carry):
        for a in (0, 1):
            ref = w_out.at[
                pl.ds(pl.multiple_of(128 * c, 128) + 64 * a, 64),
                pl.ds(pl.multiple_of(256 * hh, 256), 256),
            ]

            @pl.when(hh != h)
            def _():
                remote(ref, ref, a_s.at[a, hh], a_r.at[a, hh], sib).wait_recv()

            @pl.when(hh == h)
            def _():
                pltpu.make_async_copy(ref, ref, a_l.at[a]).wait()

        out_to_sib(hh).start()
        return carry

    lax.fori_loop(0, 16, take_out, 0)

    for u in units:
        g1(u, 0, -1).wait_recv()
        if u % 2 == 0:
            g1(u, 2, -1).start()
        g2_start(u, 1)
        g1(u, 1, 1).wait_recv()
        if u % 2 == 1:
            g1(u, 2, 1).start()
        g2_start(u, 2)
    for u in units:
        g1(u, 2, 2).wait_recv()
        g2_start(u, 3)

    def out_from_sib(hh, carry):
        ref = own_out(1 - c, hh)
        remote(ref, ref, ws.at[hh], wr.at[hh], sib).wait_recv()
        return carry

    for j in range(4):
        for u in units:
            g2(u, j, 0, -1).wait_recv()
            if u % 2 == 0:
                g2(u, j, 2, -1).start()
            g2(u, j, 1, 1).wait_recv()
            if u % 2 == 1:
                g2(u, j, 2, 1).start()

    lax.fori_loop(0, 16, out_from_sib, 0)
    for u in units:
        for j in range(4):
            g2(u, j, 2, 2).wait_recv()
        tokens = slice(128 * u, 128 * u + 128)
        value = lax.dot_general(
            gath[tokens, :], w_out[...], (((1,), (1,)), ((), ())), preferred_element_type=F32
        )

        def square(i, total):
            g = gath[tokens, pl.ds(pl.multiple_of(128 * i, 128), 128)].astype(F32)
            return total + g * g

        squares = lax.fori_loop(0, 32, square, jnp.zeros((128, 128), F32))
        mean = jnp.sum(squares, axis=1, keepdims=True) / INNER
        out_ref[tokens, :] = (value * lax.rsqrt(mean + 1e-5)).astype(BF16)

    for p in range(7):
        for d in (0, 1):

            def drain(k, carry):
                ring(p, d, k, k + 1).wait_send()
                return carry

            lax.fori_loop(0, FAR[p][d], drain, 0)
            if p < 5:

                def drain_sib(k, carry):
                    to_sib(p, d, k).wait_send()
                    return carry

                lax.fori_loop(d, FAR[p][d] + 1, drain_sib, 0)

    def drain_out(zz, carry):
        @pl.when(zz != h)
        def _():
            for p in (5, 6):
                to_owner(p, zz)[0].wait_send()

        out_to_sib(zz).wait_send()
        return carry

    lax.fori_loop(0, 16, drain_out, 0)
    for d, k, hop in sent:
        t_send(d, k, hop).wait_send()
    for u in units:
        g1(u, 0, 0).wait_send()
        g1(u, 1, 0).wait_send()
        g1(u, 2, -1 if u % 2 == 0 else 1).wait_send()
        for j in range(4):
            g2(u, j, 0, 0).wait_send()
            g2(u, j, 1, 0).wait_send()
            g2(u, j, 2, -1 if u % 2 == 0 else 1).wait_send()


def local(
    activations,
    w_inner,
    w_gate,
    w_groups,
    w_step,
    w_out,
    conv_inner,
    conv_groups,
    step_bias,
    decay_log,
    skip_gain,
    norm_gain,
):
    anywhere = pl.BlockSpec(memory_space=pl.ANY)
    vmem = pl.BlockSpec(memory_space=pltpu.VMEM)
    smem = pl.BlockSpec(memory_space=pltpu.SMEM)
    dma = pltpu.SemaphoreType.DMA
    return pl.pallas_call(
        kernel,
        out_shape=jax.ShapeDtypeStruct((TOK, 256), BF16),
        in_specs=[anywhere] * 3 + [vmem] * 5 + [smem] * 3 + [vmem],
        out_specs=vmem,
        scratch_shapes=[
            pltpu.VMEM((HALO + TOK, 4096), BF16),
            pltpu.VMEM((4096, 256), BF16),
            pltpu.VMEM((4096, 256), BF16),
            pltpu.VMEM((80, 4096), BF16),
            pltpu.VMEM((16, 128, 256), BF16),
            pltpu.VMEM((256, 4096), BF16),
            pltpu.VMEM((TOK, 4096), BF16),
            pltpu.VMEM((HALO + TOK, 256), F32),
            pltpu.VMEM((TOK, 256), F32),
            pltpu.VMEM((HALO + TOK, 80), F32),
            pltpu.VMEM((256, TOK), BF16),
            pltpu.VMEM((TOK, 256), BF16),
            pltpu.VMEM((TOK, 128), F32),
            pltpu.VMEM((144, 256), BF16),
            pltpu.VMEM((144, 256), BF16),
            pltpu.VMEM((16, 144, 128), BF16),
            pltpu.VMEM((128, 128), F32),
            pltpu.VMEM((128, 128), F32),
            dma((3,)),
            dma((2,)),
            dma((7, 2, 9)),
            dma((7, 2, 9)),
            dma((5, 2, 9)),
            dma((5, 2, 9)),
            dma((2, 16)),
            dma((2, 16)),
            dma((2,)),
            dma((16,)),
            dma((16,)),
            dma((3,)),
            dma((3,)),
            dma((4,)),
            dma((2, 2, 9)),
            dma((2, 9)),
            dma((4, 3)),
            dma((4, 3)),
            dma((4, 4, 3)),
            dma((4, 4, 3)),
        ],
        compiler_params=pltpu.CompilerParams(
            collective_id=0, has_side_effects=True, vmem_limit_bytes=48 * 1024 * 1024
        ),
    )(
        activations,
        w_inner,
        w_gate,
        w_out,
        w_groups,
        w_step,
        conv_inner,
        conv_groups,
        step_bias,
        decay_log,
        skip_gain,
        norm_gain.reshape(1, 256),
    )


def solution(mesh):
    in_specs = (
        P("seq", None),
        P("seq", "hid"),
        P("seq", "hid"),
        P("seq", None),
        P("seq", None),
        P("seq", "hid"),
        P(None, "hid"),
        P(),
        P("hid"),
        P("hid"),
        P("hid"),
        P("hid"),
    )
    return jax.shard_map(
        local, mesh=mesh, in_specs=in_specs, out_specs=P("seq", "hid"), check_vma=False
    )
```

time: 483 us -> 142 us (0.29)
  the two profiles are of different devices: /device:TPU:1 before, /device:TPU:4 now
where the time goes in v1:
time: 142 us
  Pallas kernels  131 us (92%)
  local copies, waits for them, and re-layouts  11.2 us (8%)
    pallas_call x1, Pallas kernels, local(): pl.pallas_call(kernel, out_shape=jax.ShapeDtypeStruct((TOK, 256), BF16),...  131 us
    unnamed x24, local copies, waits for them, and re-layouts  11.2 us

profile of v1, /device:TPU:4, one launch (start us, length us, event | category | flops | bytes accessed | tf_op | source)
XLA Modules:
  0.0 141.9 jit_solution(9225035053335025756)
XLA Ops:
  0.0 0.8 copy.13.wst_ref
  0.8 0.0 copy-start
  0.8 2.2 %copy-done = bf16[512,4096]{1,0:T(8,128)(2,1)S(1)} copy-done((bf16[512,4096]{1,0:T(8,128)(2,1)S(1)}, bf16[512,4096]{1,0:T(8,128)(2,1)}, u32[]{:S(2)}) %copy-start) | copy-done | bytes 4194328
  3.0 0.0 copy-start.1
  3.0 0.9 copy-done.1
  4.0 0.0 copy-start.2
  4.0 0.8 copy-done.2
  4.8 0.0 copy-start.3
  4.8 0.8 copy-done.3
  5.7 0.0 copy-start.4
  5.7 0.8 copy-done.4
  6.5 0.0 copy-start.5
  6.5 0.7 copy-done.5
  7.2 0.0 copy-start.6
  7.2 0.7 copy-done.6
  7.9 0.0 copy-start.7
  7.9 0.7 copy-done.7
  8.6 0.0 copy-start.8
  8.6 0.7 copy-done.8
  9.2 0.0 copy-start.9
  9.2 0.7 copy-done.9
  9.9 0.0 copy-start.10
  9.9 0.7 copy-done.10
  10.5 130.6 %shard_map.118 = bf16[512,256]{1,0:T(8,128)(2,1)S(1)} custom-call(bf16[512,4096]{1,0:T(8,128)(2,1)S(1)} %copy-done, bf16[128,256]{1,0:T(8,128)(2,1)S(1)} %copy-done.2, bf16[128,256]{1,0:T(8,128)(2,1)S(1)} %copy-done.3, bf16[128,256]{1,0:T(8,128)(2,1)S(1)} %copy-done.4, bf16[128,1024]{1,0:T(8,128)(2,1)S(1)} %copy-done.1, bf16[128,64]{1,0:T(8,128)(2,1)S(1)} %copy.13.wst_ref, ...), custom_call_target="tpu_custom_call" | custom-call | tf_op jit(solution)/shard_map/pallas_call | solution.py:674
  141.2 0.7 copy.15
Async XLA Ops:
  0.8 2.2 %copy-start = (bf16[512,4096]{1,0:T(8,128)(2,1)S(1)}, bf16[512,4096]{1,0:T(8,128)(2,1)}, u32[]{:S(2)}) copy-start(bf16[512,4096]{1,0:T(8,128)(2,1)} %act_hbm.1) | copy-start | bytes 12582916
  3.0 0.9 copy-start.1
  4.0 0.8 copy-start.2
  4.8 0.8 copy-start.3
  5.7 0.8 copy-start.4
  6.5 0.7 copy-start.5
  7.2 0.7 copy-start.6
  7.9 0.7 copy-start.7
  8.6 0.7 copy-start.8
  9.2 0.7 copy-start.9
  9.9 0.7 copy-start.10

commit v2 on v1

--- a/solution.py
+++ b/solution.py
@@ -10,7 +10,7 @@
 MESH = pl.DeviceIdType.MESH
 INNER = 4096
 TOK = 512
-HALO = 16
+HALO = 8
 NZ = 16
 FAR = ((8, 7), (8, 7), (7, 8), (8, 7), (7, 8), (8, 7), (7, 8))
 
@@ -30,6 +30,16 @@
     act_hbm,
     wi_hbm,
     wg_hbm,
+    wo_hbm,
+    wgr_hbm,
+    wst_hbm,
+    tapi_hbm,
+    tapg_hbm,
+    bias_hbm,
+    decay_hbm,
+    skip_hbm,
+    gain_hbm,
+    out_ref,
     wo_ref,
     wgr_ref,
     wst_ref,
@@ -39,7 +49,7 @@
     decay_ref,
     skip_ref,
     gain_ref,
-    out_ref,
+    small_sem,
     act,
     w_in,
     w_gate,
@@ -47,6 +57,18 @@
     land,
     w_out,
     gath,
+    sq_own,
+    sq_in,
+    p_up,
+    p_down,
+    p_own,
+    s_far,
+    s_up,
+    s_down,
+    r_up,
+    r_down,
+    f_up,
+    f_down,
     acc_i,
     acc_g,
     acc_s,
@@ -74,10 +96,12 @@
     es,
     ts,
     tr,
-    g1s,
-    g1r,
-    g2s,
-    g2r,
+    gs,
+    gr,
+    qs,
+    qr,
+    hs,
+    hr,
 ):
     s = lax.axis_index("seq")
     h = lax.axis_index("hid")
@@ -103,7 +127,26 @@
     own_rows = pl.ds(pl.multiple_of(s * 128, 128), 128)
     load_in = pltpu.make_async_copy(wi_hbm, w_in.at[own_rows, :], local_sem.at[1])
     load_gate = pltpu.make_async_copy(wg_hbm, w_gate.at[own_rows, :], local_sem.at[2])
+    group_cols = pl.ds(pl.multiple_of(x * 256 + (y // 2) * 128, 128), 128)
+    small = [
+        pltpu.make_async_copy(src, dst, small_sem.at[i])
+        for i, (src, dst) in enumerate(
+            (
+                (wgr_hbm.at[:, group_cols], wgr_ref),
+                (wst_hbm, wst_ref),
+                (wo_hbm, wo_ref),
+                (gain_hbm, gain_ref),
+                (tapi_hbm, tapi_ref),
+                (tapg_hbm.at[:, group_cols], tapg_ref),
+                (bias_hbm, bias_ref),
+                (decay_hbm, decay_ref),
+                (skip_hbm, skip_ref),
+            )
+        )
+    ]
     load_in.start()
+    for item in small:
+        item.start()
     load_gate.start()
     load_act.start()
 
@@ -112,14 +155,15 @@
         pl.semaphore_signal(barrier, inc=1, device_id=dev(zmod(z + step), c, h), device_id_type=MESH)
     pl.semaphore_signal(barrier, inc=1, device_id=sib, device_id_type=MESH)
     pl.semaphore_signal(barrier, inc=1, device_id=extra, device_id_type=MESH)
-    for step in range(1, 16):
-        pl.semaphore_signal(
-            barrier, inc=1, device_id=dev(z, c, lax.rem(h + step, 16)), device_id_type=MESH
-        )
-
-    tile = wgr_ref[:, pl.ds(pl.multiple_of(x * 256 + (y // 2) * 128, 128), 128)].astype(F32).T
+    for step in (1, 2, 3):
+        for hh in (hid_at(step, 0), hid_at(0, step)):
+            pl.semaphore_signal(barrier, inc=1, device_id=dev(z, c, hh), device_id_type=MESH)
+
+    for item in small:
+        item.wait()
+    tile = wgr_ref[...].astype(F32).T
     half = jnp.where(y % 2 == 0, tile[:64], tile[64:])
-    steps_t = jnp.concatenate([wst_ref[...].astype(F32)] * 2, axis=1).T
+    steps_t = wst_ref[...].astype(F32)
     mine = jnp.where(
         x < 2,
         jnp.where(x == 0, steps_t[0:16], steps_t[16:32]),
@@ -130,7 +174,7 @@
     w_gs[64:80, own_lanes] = mine.astype(BF16)
     land[z] = (wo_ref[...].astype(F32) * gain_ref[...]).astype(BF16)
 
-    pl.semaphore_wait(barrier, 21)
+    pl.semaphore_wait(barrier, 12)
 
     send_halo = remote(
         act_hbm.at[pl.ds(TOK - HALO, HALO), :],
@@ -176,13 +220,18 @@
         ref = sib_block(p, origin(d, k))
         remote(ref, ref, bs.at[p, d, k], br.at[p, d, k], sib).wait_recv()
 
+    def out_part(a, quarter, cc, column):
+        row = pl.multiple_of(256 * quarter + 128 * cc, 128) + 64 * a
+        return w_out.at[pl.ds(row, 64), pl.ds(pl.multiple_of(256 * column, 256), 256)]
+
     def to_owner(p, zz):
         a = p - 5
-        dst = w_out.at[
-            pl.ds(pl.multiple_of(128 * c, 128) + 64 * a, 64), pl.ds(pl.multiple_of(256 * h, 256), 256)
-        ]
-        return remote(block(p, zz), dst, a_s.at[a, zz], a_r.at[a, h], dev(z, c, zz)), (
-            pltpu.make_async_copy(block(p, zz), dst, a_l.at[a])
+        return (
+            block(p, zz),
+            out_part(a, zz % 4, c, x),
+            a_s.at[a, zz],
+            a_r.at[a, zz % 4, x],
+            dev(z, c, (zz // 4) * 4 + y),
         )
 
     def hand_on(p, d, k):
@@ -190,15 +239,14 @@
             to_sib(p, d, k).start()
         else:
             zz = origin(d, k)
-            far, near = to_owner(p, zz)
-
-            @pl.when(zz != h)
+
+            @pl.when(zz // 4 != x)
             def _():
-                far.start()
-
-            @pl.when(zz == h)
+                remote(*to_owner(p, zz)).start()
+
+            @pl.when(zz // 4 == x)
             def _():
-                near.start()
+                pltpu.make_async_copy(*to_owner(p, zz)[:2], a_l.at[p - 5, zz % 4]).start()
 
     def first(p):
         ring(p, 0, 0, 1).start()
@@ -211,12 +259,14 @@
             ring(p, d, k, k + 1).start()
         hand_on(p, d, k)
 
-    def dots(zz):
+    def dots_in(zz):
         col = pl.ds(pl.multiple_of(zz * 256, 256), 256)
-        a = act[:, col]
-        acc_i[...] += jnp.dot(a, w_in[col, :], preferred_element_type=F32)
+        acc_i[...] += jnp.dot(act[:, col], w_in[col, :], preferred_element_type=F32)
+
+    def dots_gs(zz):
+        col = pl.ds(pl.multiple_of(zz * 256, 256), 256)
         acc_s[...] += lax.dot_general(
-            a, w_gs[:, col], (((1,), (1,)), ((), ())), preferred_element_type=F32
+            act[:, col], w_gs[:, col], (((1,), (1,)), ((), ())), preferred_element_type=F32
         )
 
     def gate_dots(zz):
@@ -230,74 +280,65 @@
     send_halo.start()
     load_gate.wait()
     first(3)
-    load_act.wait()
-    send_halo.wait()
+    first(4)
     acc_i[...] = jnp.zeros_like(acc_i)
     acc_s[...] = jnp.zeros_like(acc_s)
     acc_g[...] = jnp.zeros_like(acc_g)
 
-    def lead(k, last):
-        for p in (0, 1, 2):
+    def serve(pieces, k):
+        for p in pieces:
             for d in (0, 1):
-                event(p, d, k, k < FAR[p][d] if last else True)
-
-    def behind(k):
-        for p in (0, 1, 2):
-            for d in (0, 1):
-                from_sib(p, d, k)
-        dots(origin(0, k))
-        dots(origin(1, k))
-
-    lead(1, False)
+                if k <= FAR[p][d]:
+                    event(p, d, k, k < FAR[p][d])
+
+    def use(pieces, dots, k, ways=(0, 1)):
+        for d in ways:
+            arrived = [p for p in pieces for e in (0, 1) if k <= FAR[p][e] and (e == d or k == 8)]
+            if k == 8 and d == 1:
+                continue
+            for p in arrived:
+                from_sib(p, d if k < 8 else (0 if FAR[p][0] == 8 else 1), k)
+            dots(origin(d, k))
+
+    IN = (1, 2)
+    GATE = (3, 4)
+    OUT = (5, 6)
+
+    serve((0,), 1)
+    serve(IN, 1)
+    load_act.wait()
+    send_halo.wait()
     for p in (0, 1, 2):
         from_sib(p, 0, 0)
-    dots(z)
-
-    def body(k, carry):
-        lead(k, False)
-        for d in (0, 1):
-            event(3, d, k - 1, True)
-        behind(k - 1)
-        return carry
-
-    lax.fori_loop(2, 7, body, 0)
-    lead(7, True)
-    for d in (0, 1):
-        event(3, d, 6, True)
-    first(4)
-    behind(6)
-    first(5)
-    first(6)
-    for p in (0, 1, 2):
-        event(p, 0 if FAR[p][0] == 8 else 1, 8, False)
-    event(3, 0, 7, True)
-    event(3, 1, 7, False)
-    behind(7)
-    for p in (0, 1, 2):
-        from_sib(p, 0 if FAR[p][0] == 8 else 1, 8)
-    dots(zmod(z + 8))
-
-    def serve(k, last=False):
-        for p in (4, 5, 6):
-            for d in (0, 1):
-                if not last:
-                    event(p, d, k, True)
-                elif k <= FAR[p][d]:
-                    event(p, d, k, k < FAR[p][d])
-
-    def gate_behind(k):
-        for p in (3, 4):
-            for d in (0, 1):
-                from_sib(p, d, k)
-        gate_dots(origin(0, k))
-        gate_dots(origin(1, k))
+    dots_gs(z)
+    dots_in(z)
+    for k in (2, 3, 4, 5, 6):
+        if k % 2 == 0:
+            serve((0,), (2, 5, 8)[k // 2 - 1])
+        serve((1,), k)
+        use((0,), dots_gs, k - 1)
+        if k % 2 == 1:
+            serve((0,), (4, 7)[k // 2 - 1])
+        use(IN, dots_in, k - 1, (0,))
+        serve((2,), k)
+        use(IN, dots_in, k - 1, (1,))
+        serve(GATE, k - 1)
+        if k in (2, 4):
+            serve((0,), (3, 6)[k // 2 - 1])
+    use((0,), dots_gs, 6)
+    serve((1,), 7)
+    use((0,), dots_gs, 7)
+    use((0,), dots_gs, 8)
+    serve((2,), 7)
+    use(IN, dots_in, 6)
+    serve(GATE, 6)
 
     not_first = jnp.where(s == 0, 0.0, 1.0).astype(F32)
     lane128 = lax.broadcasted_iota(jnp.int32, (TOK, 128), 1)
     raw = acc_s[HALO:, :]
     acc_s[...] = acc_s[...].astype(BF16).astype(F32)
     acc_s[0:HALO, :] = acc_s[0:HALO, :] * not_first
-    tap_tile = tapg_ref[:, pl.ds(pl.multiple_of(x * 256 + (y // 2) * 128, 128), 128)]
+    tap_tile = tapg_ref[...]
     tap_g = jnp.where(y % 2 == 0, tap_tile, pltpu.roll(tap_tile, 64, axis=1))
     conv = jnp.zeros((TOK, 80), F32)
     for position in range(4):
@@ -315,8 +356,11 @@
     for j in (1, 3, 2):
         y_copy(j, y).start()
 
-    serve(1)
-    event(3, 0, 8, False)
+    first(5)
+    first(6)
+    serve(IN, 8)
+    use(IN, dots_in, 7)
+    serve(GATE, 7)
 
     step4 = jnp.where(
         y < 2,
@@ -350,6 +394,8 @@
             halves.append(jnp.where(lane128 < 64, lo, hi))
         return jnp.concatenate(halves, axis=1)
 
+    use(IN, dots_in, 8)
+    serve(GATE, 8)
     acc_i[...] = acc_i[...].astype(BF16).astype(F32)
     acc_i[0:HALO, :] = acc_i[0:HALO, :] * not_first
     conv = jnp.zeros((TOK, 256), F32)
@@ -357,8 +403,6 @@
         conv = conv + acc_i[pl.ds(HALO - 3 + position, TOK), :] * tapi_ref[position : position + 1, :]
     conv = conv * jax.nn.sigmoid(conv)
     xc[...] = conv.astype(BF16)
-
-    serve(2)
 
     head_lane = lax.broadcasted_iota(jnp.int32, (1, 256), 1) // 64
     weighted = (xc[...].astype(F32) * expand(1)).astype(BF16)
@@ -380,7 +424,7 @@
     swap = remote(e_own, e_sib, es.at[0], es.at[1], sib)
     swap.start()
 
-    serve(3)
+    serve(OUT, 1)
     swap.wait()
 
     end_sib = e_sib[0:128, :].astype(F32)
@@ -439,7 +483,7 @@
         t_recv(d, 2)
         for hop in (2, 1):
             t_start(d, 2, hop)
-    serve(4)
+    serve(OUT, 2)
     mixed1 = span(1)
     skip = jnp.where(
         head_lane < 2,
@@ -453,23 +497,20 @@
         t_recv(d, 4)
         for hop in (2, 1):
             t_start(d, 4, hop)
-    serve(5)
-    for p in (3, 4):
+    serve(OUT, 3)
+    for p in GATE:
         from_sib(p, 0, 0)
     gate_dots(z)
-    for k in (1, 2):
-        gate_behind(k)
+    for k in (1, 2, 3, 4):
+        use(GATE, gate_dots, k)
     t_recv(0, 6)
     for hop in (2, 1):
         t_start(0, 6, hop)
     t_recv(1, 6)
     t_start(1, 6, 1)
-    serve(6)
-    for k in (3, 4):
-        gate_behind(k)
-    serve(7, True)
-    for k in (5, 6):
-        gate_behind(k)
+    serve(OUT, 4)
+    for k in (5, 6, 7, 8):
+        use(GATE, gate_dots, k)
     for d, ks in ((0, (1, 3, 5, 7, 8)), (1, (1, 3, 5, 7))):
         for k in ks:
             t_recv(d, k)
@@ -483,11 +524,7 @@
     pbuf[...] = prefix
     swap2 = remote(pbuf, psib, es.at[2], es.at[3], sib)
     swap2.start()
-    serve(8, True)
-    gate_behind(7)
-    for p in (3, 4):
-        from_sib(p, 0 if FAR[p][0] == 8 else 1, 8)
-    gate_dots(zmod(z + 8))
+    serve(OUT, 5)
     swap2.wait()
     other = psib[...]
     before = jnp.where(
@@ -505,152 +542,202 @@
         inter = inter + jnp.dot(c_mat[tokens], low, preferred_element_type=F32)
         mixed = mixed + inter * expcum[tokens]
         gate = acc_g[tokens, :].astype(BF16).astype(F32)
-        gath[tokens, pl.ds(pl.multiple_of(256 * h, 256), 256)] = (
+        gath[tokens, pl.ds(pl.multiple_of(256 * x, 256), 256)] = (
             mixed * (gate * jax.nn.sigmoid(gate))
         ).astype(BF16)
 
     gated(0, mixed0, state0)
     gated(1, mixed1, state1)
 
-    def offset(u, a, b):
-        return hid_at(a, b) if u < 2 else hid_at(b, a)
-
-    def part(u, a, b):
-        return gath.at[
-            pl.ds(128 * u, 128), pl.ds(pl.multiple_of(256 * offset(u, a, b), 256), 256)
+    def part(u, a, first_row, rows):
+        column = pl.multiple_of(256 * lax.rem(x + a + 4, 4), 256)
+        return gath.at[pl.ds(128 * u + first_row, rows), pl.ds(column, 256)]
+
+    STEP = (1, -1)
+
+    def g_near(u, way, a):
+        ref = part(u, a, 0, 128)
+        return remote(ref, ref, gs.at[u, way], gr.at[u, way], dev(z, c, hid_at(STEP[way], 0)))
+
+    def g_far(u, way, a):
+        ref = part(u, a, 64 * way, 64)
+        return remote(
+            ref, ref, gs.at[u, 2 + way], gr.at[u, 2 + way], dev(z, c, hid_at(STEP[way], 0))
+        )
+
+    for u in range(4):
+        for way in (0, 1):
+            g_near(u, way, 0).start()
+
+    def out_block(cc, quarter, column):
+        return w_out.at[
+            pl.ds(pl.multiple_of(256 * quarter + 128 * cc, 128), 128),
+            pl.ds(pl.multiple_of(256 * column, 256), 256),
         ]
 
-    def g1(u, slot, a):
-        ref = part(u, a, 0)
-        step = (1, -1, 1 if u % 2 == 0 else -1)[slot]
-        return remote(ref, ref, g1s.at[u, slot], g1r.at[u, slot], dev(z, c, offset(u, step, 0)))
-
-    SIDE = (0, -1, 1, 2)
-
-    def g2(u, j, slot, b):
-        ref = part(u, SIDE[j], b)
-        step = (1, -1, 1 if u % 2 == 0 else -1)[slot]
-        return remote(ref, ref, g2s.at[u, j, slot], g2r.at[u, j, slot], dev(z, c, offset(u, 0, step)))
-
-    def g2_start(u, j):
-        g2(u, j, 0, 0).start()
-        g2(u, j, 1, 0).start()
-
-    units = (0, 2, 1, 3)
-    for u in units:
-        g1(u, 0, 0).start()
-        g1(u, 1, 0).start()
-    for u in units:
-        g2_start(u, 0)
-
-    def own_out(cc, hh):
-        return w_out.at[
-            pl.ds(pl.multiple_of(128 * cc, 128), 128), pl.ds(pl.multiple_of(256 * hh, 256), 256)
-        ]
-
-    def out_to_sib(hh):
-        return remote(own_out(c, hh), own_out(c, hh), ws.at[hh], wr.at[hh], sib)
-
-    def take_out(hh, carry):
+    def out_to_sib(i):
+        ref = out_block(c, i // 4, i % 4)
+        return remote(ref, ref, ws.at[i], wr.at[i], sib)
+
+    def take_out(i, carry):
         for a in (0, 1):
-            ref = w_out.at[
-                pl.ds(pl.multiple_of(128 * c, 128) + 64 * a, 64),
-                pl.ds(pl.multiple_of(256 * hh, 256), 256),
-            ]
-
-            @pl.when(hh != h)
+            ref = out_part(a, i // 4, c, i % 4)
+
+            @pl.when(i % 4 != x)
             def _():
-                remote(ref, ref, a_s.at[a, hh], a_r.at[a, hh], sib).wait_recv()
-
-            @pl.when(hh == h)
+                remote(ref, ref, a_s.at[a, i], a_r.at[a, i // 4, i % 4], sib).wait_recv()
+
+            @pl.when(i % 4 == x)
             def _():
-                pltpu.make_async_copy(ref, ref, a_l.at[a]).wait()
-
-        out_to_sib(hh).start()
+                pltpu.make_async_copy(ref, ref, a_l.at[a, i // 4]).wait()
+
+        out_to_sib(i).start()
         return carry
 
-    lax.fori_loop(0, 16, take_out, 0)
-
-    for u in units:
-        g1(u, 0, -1).wait_recv()
-        if u % 2 == 0:
-            g1(u, 2, -1).start()
-        g2_start(u, 1)
-        g1(u, 1, 1).wait_recv()
-        if u % 2 == 1:
-            g1(u, 2, 1).start()
-        g2_start(u, 2)
-    for u in units:
-        g1(u, 2, 2).wait_recv()
-        g2_start(u, 3)
-
-    def out_from_sib(hh, carry):
-        ref = own_out(1 - c, hh)
-        remote(ref, ref, ws.at[hh], wr.at[hh], sib).wait_recv()
+    def out_from_sib(i, carry):
+        ref = out_block(1 - c, i // 4, i % 4)
+        remote(ref, ref, ws.at[i], wr.at[i], sib).wait_recv()
         return carry
 
-    for j in range(4):
-        for u in units:
-            g2(u, j, 0, -1).wait_recv()
-            if u % 2 == 0:
-                g2(u, j, 2, -1).start()
-            g2(u, j, 1, 1).wait_recv()
-            if u % 2 == 1:
-                g2(u, j, 2, 1).start()
-
-    lax.fori_loop(0, 16, out_from_sib, 0)
-    for u in units:
-        for j in range(4):
-            g2(u, j, 2, 2).wait_recv()
-        tokens = slice(128 * u, 128 * u + 128)
-        value = lax.dot_general(
-            gath[tokens, :], w_out[...], (((1,), (1,)), ((), ())), preferred_element_type=F32
-        )
-
-        def square(i, total):
-            g = gath[tokens, pl.ds(pl.multiple_of(128 * i, 128), 128)].astype(F32)
-            return total + g * g
-
-        squares = lax.fori_loop(0, 32, square, jnp.zeros((128, 128), F32))
-        mean = jnp.sum(squares, axis=1, keepdims=True) / INNER
-        out_ref[tokens, :] = (value * lax.rsqrt(mean + 1e-5)).astype(BF16)
-
-    for p in range(7):
-        for d in (0, 1):
-
-            def drain(k, carry):
-                ring(p, d, k, k + 1).wait_send()
-                return carry
-
-            lax.fori_loop(0, FAR[p][d], drain, 0)
-            if p < 5:
-
-                def drain_sib(k, carry):
-                    to_sib(p, d, k).wait_send()
-                    return carry
-
-                lax.fori_loop(d, FAR[p][d] + 1, drain_sib, 0)
-
-    def drain_out(zz, carry):
-        @pl.when(zz != h)
+    def drain_out(i, carry):
+        @pl.when(i // 4 != x)
         def _():
             for p in (5, 6):
-                to_owner(p, zz)[0].wait_send()
-
-        out_to_sib(zz).wait_send()
+                remote(*to_owner(p, i)).wait_send()
+
+        out_to_sib(i).wait_send()
         return carry
 
+    def drain_weights():
+        for p in range(7):
+            for d in (0, 1):
+
+                def drain(k, carry):
+                    ring(p, d, k, k + 1).wait_send()
+                    return carry
+
+                lax.fori_loop(0, FAR[p][d], drain, 0)
+                if p < 5:
+
+                    def drain_sib(k, carry):
+                        to_sib(p, d, k).wait_send()
+                        return carry
+
+                    lax.fori_loop(d, FAR[p][d] + 1, drain_sib, 0)
+
+    serve(OUT, 6)
+    for u in range(4):
+        for way in (0, 1):
+            g_near(u, way, -STEP[way]).wait_recv()
+            g_far(u, way, -STEP[way]).start()
+        if u < 2:
+            serve(OUT, 7 + u)
+    lax.fori_loop(0, 16, take_out, 0)
+    drain_weights()
+    lax.fori_loop(0, 16, out_from_sib, 0)
+
+    def product(u, offset):
+        rows = pl.ds(pl.multiple_of(256 * lax.rem(y + offset, 4), 256), 256)
+        return lax.dot_general(
+            gath[128 * u : 128 * u + 128, :],
+            w_out[rows, :],
+            (((1,), (1,)), ((), ())),
+            preferred_element_type=F32,
+        )
+
+    def along(u, slot, way, src, dst):
+        return remote(
+            src, dst, hs.at[u, slot, way], hr.at[u, slot, way], dev(z, c, hid_at(0, STEP[way]))
+        )
+
+    top = pl.ds(0, 64)
+    low = pl.ds(64, 64)
+
+    def far_send(u, way):
+        return along(u, 0, way, s_far.at[u, (top, low)[way]], (r_up, r_down)[way].at[u])
+
+    def early_send(u, way):
+        rows = (low, top)[way]
+        return along(u, 1, way, (s_up, s_down)[way].at[u, rows], (f_up, f_down)[way].at[u, rows])
+
+    def late_send(u, way):
+        rows = (top, low)[way]
+        return along(u, 2, way, (s_up, s_down)[way].at[u, rows], (f_up, f_down)[way].at[u, rows])
+
+    def square_send(u, j):
+        return remote(
+            sq_own.at[u], sq_in.at[u, j - 1], qs.at[u, j - 1], qr.at[u, j - 1], dev(z, c, hid_at(0, j))
+        )
+
+    def multiply(u):
+        for way in (0, 1):
+            g_far(u, way, 2).wait_recv()
+        s_far[u] = product(u, 2).astype(BF16)
+        for way in (0, 1):
+            far_send(u, way).start()
+        up = product(u, 1)
+        s_up[u, 64:128, :] = up[64:128].astype(BF16)
+        p_up[u] = up[0:64]
+        down = product(u, 3)
+        s_down[u, 0:64, :] = down[0:64].astype(BF16)
+        p_down[u] = down[64:128]
+        for way in (0, 1):
+            early_send(u, way).start()
+        total = jnp.zeros((128, 128), F32)
+        for i in range(8):
+            g = gath[128 * u : 128 * u + 128, 128 * i : 128 * i + 128].astype(F32)
+            total = total + g * g
+        sq_own[u] = jnp.broadcast_to(jnp.sum(total.T, axis=0, keepdims=True), (8, 128))
+        for j in (1, 3, 2):
+            square_send(u, j).start()
+        p_own[u] = product(u, 0)
+
+    def add(u):
+        far_send(u, 0).wait_recv()
+        s_up[u, 0:64, :] = (p_up[u] + r_up[u].astype(F32)).astype(BF16)
+        late_send(u, 0).start()
+        far_send(u, 1).wait_recv()
+        s_down[u, 64:128, :] = (p_down[u] + r_down[u].astype(F32)).astype(BF16)
+        late_send(u, 1).start()
+
+    def finish(u):
+        for way in (0, 1):
+            early_send(u, way).wait_recv()
+            late_send(u, way).wait_recv()
+        for j in (1, 2, 3):
+            square_send(u, j).wait_recv()
+        squares = sq_own[u] + sq_in[u, 0] + sq_in[u, 1] + sq_in[u, 2]
+        scale = lax.rsqrt(squares / INNER + 1e-5)
+        scale = jnp.broadcast_to(scale[0:1], (128, 128)).T
+        value = p_own[u] + f_up[u].astype(F32) + f_down[u].astype(F32)
+        for half_of in (0, 128):
+            out_ref[128 * u : 128 * u + 128, half_of : half_of + 128] = (
+                value[:, half_of : half_of + 128] * scale
+            ).astype(BF16)
+
+    multiply(0)
+    multiply(1)
+    add(0)
+    multiply(2)
+    add(1)
+    multiply(3)
+    add(2)
+    finish(0)
     lax.fori_loop(0, 16, drain_out, 0)
     for d, k, hop in sent:
         t_send(d, k, hop).wait_send()
-    for u in units:
-        g1(u, 0, 0).wait_send()
-        g1(u, 1, 0).wait_send()
-        g1(u, 2, -1 if u % 2 == 0 else 1).wait_send()
-        for j in range(4):
-            g2(u, j, 0, 0).wait_send()
-            g2(u, j, 1, 0).wait_send()
-            g2(u, j, 2, -1 if u % 2 == 0 else 1).wait_send()
+    add(3)
+    for u in (1, 2, 3):
+        finish(u)
+    for u in range(4):
+        for way in (0, 1):
+            g_near(u, way, 0).wait_send()
+            g_far(u, way, -STEP[way]).wait_send()
+            far_send(u, way).wait_send()
+            early_send(u, way).wait_send()
+            late_send(u, way).wait_send()
+        for j in (1, 2, 3):
+            square_send(u, j).wait_send()
 
 
 def local(
@@ -669,21 +756,42 @@
 ):
     anywhere = pl.BlockSpec(memory_space=pl.ANY)
     vmem = pl.BlockSpec(memory_space=pltpu.VMEM)
-    smem = pl.BlockSpec(memory_space=pltpu.SMEM)
     dma = pltpu.SemaphoreType.DMA
     return pl.pallas_call(
         kernel,
         out_shape=jax.ShapeDtypeStruct((TOK, 256), BF16),
-        in_specs=[anywhere] * 3 + [vmem] * 5 + [smem] * 3 + [vmem],
+        in_specs=[anywhere] * 12,
         out_specs=vmem,
         scratch_shapes=[
+            pltpu.VMEM((128, 256), BF16),
+            pltpu.VMEM((128, 128), BF16),
+            pltpu.VMEM((64, 128), BF16),
+            pltpu.VMEM((4, 256), F32),
+            pltpu.VMEM((4, 128), F32),
+            pltpu.SMEM((4,), F32),
+            pltpu.SMEM((4,), F32),
+            pltpu.SMEM((4,), F32),
+            pltpu.VMEM((1, 256), F32),
+            dma((9,)),
             pltpu.VMEM((HALO + TOK, 4096), BF16),
             pltpu.VMEM((4096, 256), BF16),
             pltpu.VMEM((4096, 256), BF16),
             pltpu.VMEM((80, 4096), BF16),
             pltpu.VMEM((16, 128, 256), BF16),
-            pltpu.VMEM((256, 4096), BF16),
-            pltpu.VMEM((TOK, 4096), BF16),
+            pltpu.VMEM((1024, 1024), BF16),
+            pltpu.VMEM((TOK, 1024), BF16),
+            pltpu.VMEM((4, 8, 128), F32),
+            pltpu.VMEM((4, 3, 8, 128), F32),
+            pltpu.VMEM((4, 64, 256), F32),
+            pltpu.VMEM((4, 64, 256), F32),
+            pltpu.VMEM((4, 128, 256), F32),
+            pltpu.VMEM((4, 128, 256), BF16),
+            pltpu.VMEM((4, 128, 256), BF16),
+            pltpu.VMEM((4, 128, 256), BF16),
+            pltpu.VMEM((4, 64, 256), BF16),
+            pltpu.VMEM((4, 64, 256), BF16),
+            pltpu.VMEM((4, 128, 256), BF16),
+            pltpu.VMEM((4, 128, 256), BF16),
             pltpu.VMEM((HALO + TOK, 256), F32),
             pltpu.VMEM((TOK, 256), F32),
             pltpu.VMEM((HALO + TOK, 80), F32),
@@ -702,8 +810,8 @@
             dma((5, 2, 9)),
             dma((5, 2, 9)),
             dma((2, 16)),
-            dma((2, 16)),
-            dma((2,)),
+            dma((2, 4, 4)),
+            dma((2, 4)),
             dma((16,)),
             dma((16,)),
             dma((3,)),
@@ -711,13 +819,15 @@
             dma((4,)),
             dma((2, 2, 9)),
             dma((2, 9)),
+            dma((4, 4)),
+            dma((4, 4)),
             dma((4, 3)),
             dma((4, 3)),
-            dma((4, 4, 3)),
-            dma((4, 4, 3)),
+            dma((4, 3, 2)),
+            dma((4, 3, 2)),
         ],
         compiler_params=pltpu.CompilerParams(
-            collective_id=0, has_side_effects=True, vmem_limit_bytes=48 * 1024 * 1024
+            collective_id=0, has_side_effects=True, vmem_limit_bytes=67043328
         ),
     )(
         activations,
@@ -725,7 +835,7 @@
         w_gate,
         w_out,
         w_groups,
-        w_step,
+        w_step.T,
         conv_inner,
         conv_groups,
         step_bias,

time: 142 us -> 115 us (0.81)
  the two profiles are of different devices: /device:TPU:4 before, /device:TPU:36 now
where the time goes in v2:
time: 115 us
  Pallas kernels  113 us (98%)
  local copies, waits for them, and re-layouts  1.67 us (1%)
    pallas_call x1, Pallas kernels, local(): pl.pallas_call(kernel, out_shape=jax.ShapeDtypeStruct((TOK, 256), BF16),...  113 us

profile of v2, /device:TPU:36, one launch (start us, length us, event | category | flops | bytes accessed | tf_op | source)
XLA Modules:
  0.0 114.6 jit_solution(9909545977837868864)
XLA Ops:
  0.0 113.0 %shard_map.118 = bf16[512,256]{1,0:T(8,128)(2,1)} custom-call(bf16[512,4096]{1,0:T(8,128)(2,1)} %act_hbm.1, bf16[128,256]{1,0:T(8,128)(2,1)} %wi_hbm.1, bf16[128,256]{1,0:T(8,128)(2,1)} %wg_hbm.1, bf16[128,256]{1,0:T(8,128)(2,1)} %wo_hbm.1, bf16[128,1024]{1,0:T(8,128)(2,1)} %wgr_hbm.1, bf16[64,128]{1,0:T(8,128)(2,1)} %bitcast.2, f32[4,256]{1,0:T(4,128)} %tapi_hbm.1, ...), custom_call_target="tpu_custom_call" | custom-call | tf_op jit(solution)/shard_map/pallas_call | solution.py:760
  113.0 1.7 %copy.14 = bf16[512,256]{1,0:T(8,128)(2,1)} copy(bf16[512,256]{1,0:T(8,128)(2,1)} %shard_map.118) | data formatting | bytes 524288

commit v3 on v2

--- a/solution.py
+++ b/solution.py
@@ -12,7 +12,7 @@
 TOK = 512
 HALO = 8
 NZ = 16
-FAR = ((8, 7), (8, 7), (7, 8), (8, 7), (7, 8), (8, 7), (7, 8))
+FAR = ((8, 7), (8, 7), (7, 8), (8, 7), (7, 8))
 
 
 def remote(src, dst, send, recv, device):
@@ -86,9 +86,10 @@
     zr,
     bs,
     br,
-    a_s,
-    a_r,
-    a_l,
+    cs,
+    cr,
+    os_,
+    orr,
     ws,
     wr,
     ys,
@@ -172,7 +173,6 @@
     own_lanes = pl.ds(pl.multiple_of(s * 128, 128), 128)
     w_gs[0:64, own_lanes] = half.astype(BF16)
     w_gs[64:80, own_lanes] = mine.astype(BF16)
-    land[z] = (wo_ref[...].astype(F32) * gain_ref[...]).astype(BF16)
 
     pl.semaphore_wait(barrier, 12)
 
@@ -191,9 +191,7 @@
         part = 64 * ((p - 1) % 2)
         if p < 3:
             return w_in.at[pl.ds(row + part, 64), :]
-        if p < 5:
-            return w_gate.at[pl.ds(row + part, 64), :]
-        return land.at[zz, pl.ds(part, 64), :]
+        return w_gate.at[pl.ds(row + part, 64), :]
 
     def sib_block(p, zz):
         row = pl.multiple_of((2 * zz + 1 - c) * 128, 128)
@@ -220,33 +218,134 @@
         ref = sib_block(p, origin(d, k))
         remote(ref, ref, bs.at[p, d, k], br.at[p, d, k], sib).wait_recv()
 
-    def out_part(a, quarter, cc, column):
-        row = pl.multiple_of(256 * quarter + 128 * cc, 128) + 64 * a
-        return w_out.at[pl.ds(row, 64), pl.ds(pl.multiple_of(256 * column, 256), 256)]
-
-    def to_owner(p, zz):
-        a = p - 5
-        return (
-            block(p, zz),
-            out_part(a, zz % 4, c, x),
-            a_s.at[a, zz],
-            a_r.at[a, zz % 4, x],
-            dev(z, c, (zz // 4) * 4 + y),
+    keeper = z % 4
+    is_source = keeper == y
+
+    def out_rows(zz, cc):
+        return pl.multiple_of((zz // 4) * 256 + 128 * cc, 128)
+
+    def out_part(a, zz, cc, column):
+        return w_out.at[
+            pl.ds(out_rows(zz, cc) + 64 * a, 64), pl.ds(pl.multiple_of(256 * column, 256), 256)
+        ]
+
+    def bring(column):
+        return remote(
+            land,
+            w_out.at[pl.ds(out_rows(z, c), 128), pl.ds(pl.multiple_of(256 * column, 256), 256)],
+            cs.at[0],
+            cr.at[column],
+            dev(z, c, x * 4 + keeper),
         )
 
+    near = tuple((d + 3) % 4 + 1 for d in (z - y + 16, y - z + 16))
+    OUT_FAR = ((8, 7), (7, 8))
+
+    def out_dist(d, q):
+        return near[d] + 4 * (q // 4)
+
+    def out_origin(d, q):
+        return zmod(z - out_dist(d, q)) if d == 0 else zmod(z + out_dist(d, q))
+
+    def out_send(a, d, zz, column, slot):
+        ref = out_part(a, zz, c, column)
+        target = zmod(z + 1) if d == 0 else zmod(z - 1)
+        return remote(ref, ref, os_.at[a, d, slot], orr.at[a, d, slot], dev(target, c, h))
+
+    def out_to_sib(a, d, zz, column, slot):
+        ref = out_part(a, zz, c, column)
+        return remote(ref, ref, ws.at[a, d, slot], wr.at[a, d, slot], sib)
+
+    def next_slot(d, q):
+        return jnp.where(near[d] < 4, q, q + 4)
+
+    def serve_out(t):
+        if t == 0:
+
+            @pl.when(is_source)
+            def _():
+                for step in (1, 2, 3):
+                    bring(lax.rem(y + step, 4)).wait_recv()
+
+        if t < 4:
+
+            @pl.when(is_source)
+            def _():
+                for a in (0, 1):
+                    for d in (0, 1):
+                        out_send(a, d, z, t, t).start()
+                    out_to_sib(a, 2, z, t, t).start()
+
+        if t > 0:
+            for a in (0, 1):
+                for d in (0, 1):
+                    q = t - near[d]
+                    reach = out_dist(d, q)
+
+                    @pl.when((q >= 0) & (q < 8) & (reach <= OUT_FAR[a][d]))
+                    def _():
+                        zz, column = out_origin(d, q), q % 4
+                        out_send(a, d, zz, column, q).wait_recv()
+
+                        @pl.when(reach < OUT_FAR[a][d])
+                        def _():
+                            out_send(a, d, zz, column, next_slot(d, q)).start()
+
+                        out_to_sib(a, d, zz, column, q).start()
+
+    def out_end(q, carry):
+        for a in (0, 1):
+            for d in (0, 1):
+                reach = out_dist(d, q)
+
+                @pl.when(reach <= OUT_FAR[a][d])
+                def _():
+                    zz, column = out_origin(d, q), q % 4
+                    theirs = out_part(a, zz, 1 - c, column)
+                    remote(theirs, theirs, ws.at[a, d, q], wr.at[a, d, q], sib).wait_recv()
+
+        return carry
+
+    def out_own_end():
+        @pl.when(is_source)
+        def _():
+            for a in (0, 1):
+                for column in range(4):
+                    theirs = out_part(a, z, 1 - c, column)
+                    remote(theirs, theirs, ws.at[a, 2, column], wr.at[a, 2, column], sib).wait_recv()
+
+    def out_drain(q, carry):
+        for a in (0, 1):
+            for d in (0, 1):
+                reach = out_dist(d, q)
+
+                @pl.when(reach <= OUT_FAR[a][d])
+                def _():
+                    zz, column = out_origin(d, q), q % 4
+
+                    @pl.when(reach < OUT_FAR[a][d])
+                    def _():
+                        out_send(a, d, zz, column, next_slot(d, q)).wait_send()
+
+                    out_to_sib(a, d, zz, column, q).wait_send()
+
+        return carry
+
+    def out_own_drain():
+        @pl.when(is_source)
+        def _():
+            for a in (0, 1):
+                for column in range(4):
+                    for d in (0, 1):
+                        out_send(a, d, z, column, column).wait_send()
+                    out_to_sib(a, 2, z, column, column).wait_send()
+
+        @pl.when(jnp.logical_not(is_source))
+        def _():
+            bring(y).wait_send()
+
     def hand_on(p, d, k):
-        if p < 5:
-            to_sib(p, d, k).start()
-        else:
-            zz = origin(d, k)
-
-            @pl.when(zz // 4 != x)
-            def _():
-                remote(*to_owner(p, zz)).start()
-
-            @pl.when(zz // 4 == x)
-            def _():
-                pltpu.make_async_copy(*to_owner(p, zz)[:2], a_l.at[p - 5, zz % 4]).start()
+        to_sib(p, d, k).start()
 
     def first(p):
         ring(p, 0, 0, 1).start()
@@ -259,19 +358,31 @@
             ring(p, d, k, k + 1).start()
         hand_on(p, d, k)
 
-    def dots_in(zz):
-        col = pl.ds(pl.multiple_of(zz * 256, 256), 256)
-        acc_i[...] += jnp.dot(act[:, col], w_in[col, :], preferred_element_type=F32)
-
-    def dots_gs(zz):
-        col = pl.ds(pl.multiple_of(zz * 256, 256), 256)
-        acc_s[...] += lax.dot_general(
-            act[:, col], w_gs[:, col], (((1,), (1,)), ((), ())), preferred_element_type=F32
+    def columns(zz):
+        return pl.ds(pl.multiple_of(zz * 256, 256), 256)
+
+    def dots_in(*planes):
+        acc_i[...] += sum(
+            jnp.dot(act[:, columns(zz)], w_in[columns(zz), :], preferred_element_type=F32)
+            for zz in planes
         )
 
-    def gate_dots(zz):
-        col = pl.ds(pl.multiple_of(zz * 256, 256), 256)
-        acc_g[...] += jnp.dot(act[HALO:, col], w_gate[col, :], preferred_element_type=F32)
+    def dots_gs(*planes):
+        acc_s[...] += sum(
+            lax.dot_general(
+                act[:, columns(zz)],
+                w_gs[:, columns(zz)],
+                (((1,), (1,)), ((), ())),
+                preferred_element_type=F32,
+            )
+            for zz in planes
+        )
+
+    def gate_dots(*planes):
+        acc_g[...] += sum(
+            jnp.dot(act[HALO:, columns(zz)], w_gate[columns(zz), :], preferred_element_type=F32)
+            for zz in planes
+        )
 
     first(0)
     load_in.wait()
@@ -280,7 +391,17 @@
     send_halo.start()
     load_gate.wait()
     first(3)
-    first(4)
+    scaled = (wo_ref[...].astype(F32) * gain_ref[...]).astype(BF16)
+
+    @pl.when(is_source)
+    def _():
+        w_out[pl.ds(out_rows(z, c), 128), pl.ds(pl.multiple_of(256 * y, 256), 256)] = scaled
+
+    @pl.when(jnp.logical_not(is_source))
+    def _():
+        land[...] = scaled
+        bring(y).start()
+
     acc_i[...] = jnp.zeros_like(acc_i)
     acc_s[...] = jnp.zeros_like(acc_s)
     acc_g[...] = jnp.zeros_like(acc_g)
@@ -291,18 +412,18 @@
                 if k <= FAR[p][d]:
                     event(p, d, k, k < FAR[p][d])
 
-    def use(pieces, dots, k, ways=(0, 1)):
-        for d in ways:
-            arrived = [p for p in pieces for e in (0, 1) if k <= FAR[p][e] and (e == d or k == 8)]
-            if k == 8 and d == 1:
-                continue
-            for p in arrived:
-                from_sib(p, d if k < 8 else (0 if FAR[p][0] == 8 else 1), k)
-            dots(origin(d, k))
+    def use(pieces, dots, k):
+        for p in pieces:
+            for d in (0, 1):
+                if k <= FAR[p][d]:
+                    from_sib(p, d, k)
+        if k < 8:
+            dots(origin(0, k), origin(1, k))
+        else:
+            dots(origin(0, k))
 
     IN = (1, 2)
     GATE = (3, 4)
-    OUT = (5, 6)
 
     serve((0,), 1)
     serve(IN, 1)
@@ -312,26 +433,17 @@
         from_sib(p, 0, 0)
     dots_gs(z)
     dots_in(z)
-    for k in (2, 3, 4, 5, 6):
-        if k % 2 == 0:
-            serve((0,), (2, 5, 8)[k // 2 - 1])
-        serve((1,), k)
+    for k in (2, 3, 4, 5, 6, 7):
+        serve((0, 1), k)
         use((0,), dots_gs, k - 1)
-        if k % 2 == 1:
-            serve((0,), (4, 7)[k // 2 - 1])
-        use(IN, dots_in, k - 1, (0,))
         serve((2,), k)
-        use(IN, dots_in, k - 1, (1,))
-        serve(GATE, k - 1)
-        if k in (2, 4):
-            serve((0,), (3, 6)[k // 2 - 1])
-    use((0,), dots_gs, 6)
-    serve((1,), 7)
+        use(IN, dots_in, k - 1)
+        serve((3,), k - 1)
+    serve((0,), 8)
+    first(4)
+    serve_out(0)
     use((0,), dots_gs, 7)
     use((0,), dots_gs, 8)
-    serve((2,), 7)
-    use(IN, dots_in, 6)
-    serve(GATE, 6)
 
     not_first = jnp.where(s == 0, 0.0, 1.0).astype(F32)
     lane128 = lax.broadcasted_iota(jnp.int32, (TOK, 128), 1)
@@ -356,11 +468,9 @@
     for j in (1, 3, 2):
         y_copy(j, y).start()
 
-    first(5)
-    first(6)
     serve(IN, 8)
+    serve((3,), 7)
     use(IN, dots_in, 7)
-    serve(GATE, 7)
 
     step4 = jnp.where(
         y < 2,
@@ -395,7 +505,9 @@
         return jnp.concatenate(halves, axis=1)
 
     use(IN, dots_in, 8)
-    serve(GATE, 8)
+    serve((3,), 8)
+    serve((4,), 1)
+    serve_out(1)
     acc_i[...] = acc_i[...].astype(BF16).astype(F32)
     acc_i[0:HALO, :] = acc_i[0:HALO, :] * not_first
     conv = jnp.zeros((TOK, 256), F32)
@@ -424,7 +536,8 @@
     swap = remote(e_own, e_sib, es.at[0], es.at[1], sib)
     swap.start()
 
-    serve(OUT, 1)
+    serve((4,), 2)
+    serve_out(2)
     swap.wait()
 
     end_sib = e_sib[0:128, :].astype(F32)
@@ -479,12 +592,15 @@
         return total
 
     mixed0 = span(0)
+    serve((4,), 3)
+    serve_out(3)
     for d in (0, 1):
         t_recv(d, 2)
         for hop in (2, 1):
             t_start(d, 2, hop)
-    serve(OUT, 2)
+    serve((4,), 4)
     mixed1 = span(1)
+    serve_out(4)
     skip = jnp.where(
         head_lane < 2,
         jnp.where(head_lane == 0, skip_ref[0], skip_ref[1]),
@@ -497,7 +613,8 @@
         t_recv(d, 4)
         for hop in (2, 1):
             t_start(d, 4, hop)
-    serve(OUT, 3)
+    serve((4,), 5)
+    serve_out(5)
     for p in GATE:
         from_sib(p, 0, 0)
     gate_dots(z)
@@ -508,9 +625,12 @@
         t_start(0, 6, hop)
     t_recv(1, 6)
     t_start(1, 6, 1)
-    serve(OUT, 4)
-    for k in (5, 6, 7, 8):
-        use(GATE, gate_dots, k)
+    serve((4,), 6)
+    serve_out(6)
+    use(GATE, gate_dots, 5)
+    serve((4,), 7)
+    serve_out(7)
+    use(GATE, gate_dots, 6)
     for d, ks in ((0, (1, 3, 5, 7, 8)), (1, (1, 3, 5, 7))):
         for k in ks:
             t_recv(d, k)
@@ -524,7 +644,9 @@
     pbuf[...] = prefix
     swap2 = remote(pbuf, psib, es.at[2], es.at[3], sib)
     swap2.start()
-    serve(OUT, 5)
+    serve((4,), 8)
+    use(GATE, gate_dots, 7)
+    use(GATE, gate_dots, 8)
     swap2.wait()
     other = psib[...]
     before = jnp.where(
@@ -542,74 +664,44 @@
         inter = inter + jnp.dot(c_mat[tokens], low, preferred_element_type=F32)
         mixed = mixed + inter * expcum[tokens]
         gate = acc_g[tokens, :].astype(BF16).astype(F32)
-        gath[tokens, pl.ds(pl.multiple_of(256 * x, 256), 256)] = (
+        gath[tokens, pl.ds(pl.multiple_of(256 * y, 256), 256)] = (
             mixed * (gate * jax.nn.sigmoid(gate))
         ).astype(BF16)
 
-    gated(0, mixed0, state0)
-    gated(1, mixed1, state1)
-
     def part(u, a, first_row, rows):
-        column = pl.multiple_of(256 * lax.rem(x + a + 4, 4), 256)
+        column = pl.multiple_of(256 * lax.rem(y + a + 4, 4), 256)
         return gath.at[pl.ds(128 * u + first_row, rows), pl.ds(column, 256)]
 
     STEP = (1, -1)
 
     def g_near(u, way, a):
         ref = part(u, a, 0, 128)
-        return remote(ref, ref, gs.at[u, way], gr.at[u, way], dev(z, c, hid_at(STEP[way], 0)))
+        return remote(ref, ref, gs.at[u, way], gr.at[u, way], dev(z, c, hid_at(0, STEP[way])))
 
     def g_far(u, way, a):
         ref = part(u, a, 64 * way, 64)
         return remote(
-            ref, ref, gs.at[u, 2 + way], gr.at[u, 2 + way], dev(z, c, hid_at(STEP[way], 0))
+            ref, ref, gs.at[u, 2 + way], gr.at[u, 2 + way], dev(z, c, hid_at(0, STEP[way]))
         )
 
-    for u in range(4):
+    def near_start(u):
         for way in (0, 1):
             g_near(u, way, 0).start()
 
-    def out_block(cc, quarter, column):
-        return w_out.at[
-            pl.ds(pl.multiple_of(256 * quarter + 128 * cc, 128), 128),
-            pl.ds(pl.multiple_of(256 * column, 256), 256),
-        ]
-
-    def out_to_sib(i):
-        ref = out_block(c, i // 4, i % 4)
-        return remote(ref, ref, ws.at[i], wr.at[i], sib)
-
-    def take_out(i, carry):
-        for a in (0, 1):
-            ref = out_part(a, i // 4, c, i % 4)
-
-            @pl.when(i % 4 != x)
-            def _():
-                remote(ref, ref, a_s.at[a, i], a_r.at[a, i // 4, i % 4], sib).wait_recv()
-
-            @pl.when(i % 4 == x)
-            def _():
-                pltpu.make_async_copy(ref, ref, a_l.at[a, i // 4]).wait()
-
-        out_to_sib(i).start()
-        return carry
-
-    def out_from_sib(i, carry):
-        ref = out_block(1 - c, i // 4, i % 4)
-        remote(ref, ref, ws.at[i], wr.at[i], sib).wait_recv()
-        return carry
-
-    def drain_out(i, carry):
-        @pl.when(i // 4 != x)
-        def _():
-            for p in (5, 6):
-                remote(*to_owner(p, i)).wait_send()
-
-        out_to_sib(i).wait_send()
-        return carry
+    def near_take(u):
+        for way in (0, 1):
+            g_near(u, way, -STEP[way]).wait_recv()
+            g_far(u, way, -STEP[way]).start()
+
+    gated(0, mixed0, state0)
+    near_start(0)
+    near_start(1)
+    gated(1, mixed1, state1)
+    near_start(2)
+    serve_out(8)
 
     def drain_weights():
-        for p in range(7):
+        for p in range(5):
             for d in (0, 1):
 
                 def drain(k, carry):
@@ -617,29 +709,28 @@
                     return carry
 
                 lax.fori_loop(0, FAR[p][d], drain, 0)
-                if p < 5:
-
-                    def drain_sib(k, carry):
-                        to_sib(p, d, k).wait_send()
-                        return carry
-
-                    lax.fori_loop(d, FAR[p][d] + 1, drain_sib, 0)
-
-    serve(OUT, 6)
-    for u in range(4):
-        for way in (0, 1):
-            g_near(u, way, -STEP[way]).wait_recv()
-            g_far(u, way, -STEP[way]).start()
-        if u < 2:
-            serve(OUT, 7 + u)
-    lax.fori_loop(0, 16, take_out, 0)
-    drain_weights()
-    lax.fori_loop(0, 16, out_from_sib, 0)
+
+                def drain_sib(k, carry):
+                    to_sib(p, d, k).wait_send()
+                    return carry
+
+                lax.fori_loop(d, FAR[p][d] + 1, drain_sib, 0)
+
+    near_take(0)
+    near_take(1)
+    near_start(3)
+    serve_out(9)
+    near_take(2)
+    serve_out(10)
+    near_take(3)
+    serve_out(11)
+    lax.fori_loop(0, 8, out_end, 0)
+    out_own_end()
 
     def product(u, offset):
-        rows = pl.ds(pl.multiple_of(256 * lax.rem(y + offset, 4), 256), 256)
+        rows = pl.ds(pl.multiple_of(256 * lax.rem(x + offset, 4), 256), 256)
         return lax.dot_general(
-            gath[128 * u : 128 * u + 128, :],
+            gath[256 * u : 256 * u + 256, :],
             w_out[rows, :],
             (((1,), (1,)), ((), ())),
             preferred_element_type=F32,
@@ -647,11 +738,11 @@
 
     def along(u, slot, way, src, dst):
         return remote(
-            src, dst, hs.at[u, slot, way], hr.at[u, slot, way], dev(z, c, hid_at(0, STEP[way]))
+            src, dst, hs.at[u, slot, way], hr.at[u, slot, way], dev(z, c, hid_at(STEP[way], 0))
         )
 
-    top = pl.ds(0, 64)
-    low = pl.ds(64, 64)
+    top = pl.ds(0, 128)
+    low = pl.ds(128, 128)
 
     def far_send(u, way):
         return along(u, 0, way, s_far.at[u, (top, low)[way]], (r_up, r_down)[way].at[u])
@@ -666,73 +757,81 @@
 
     def square_send(u, j):
         return remote(
-            sq_own.at[u], sq_in.at[u, j - 1], qs.at[u, j - 1], qr.at[u, j - 1], dev(z, c, hid_at(0, j))
+            sq_own.at[u], sq_in.at[u, j - 1], qs.at[u, j - 1], qr.at[u, j - 1], dev(z, c, hid_at(j, 0))
         )
 
-    def multiply(u):
-        for way in (0, 1):
-            g_far(u, way, 2).wait_recv()
+    def multiply_far(u):
         s_far[u] = product(u, 2).astype(BF16)
         for way in (0, 1):
             far_send(u, way).start()
+
+    def multiply_near(u):
         up = product(u, 1)
-        s_up[u, 64:128, :] = up[64:128].astype(BF16)
-        p_up[u] = up[0:64]
+        s_up[u, 128:256, :] = up[128:256].astype(BF16)
+        early_send(u, 0).start()
+        p_up[u] = up[0:128]
         down = product(u, 3)
-        s_down[u, 0:64, :] = down[0:64].astype(BF16)
-        p_down[u] = down[64:128]
-        for way in (0, 1):
-            early_send(u, way).start()
-        total = jnp.zeros((128, 128), F32)
+        s_down[u, 0:128, :] = down[0:128].astype(BF16)
+        early_send(u, 1).start()
+        p_down[u] = down[128:256]
+
+    def square(u):
+        total = jnp.zeros((256, 128), F32)
         for i in range(8):
-            g = gath[128 * u : 128 * u + 128, 128 * i : 128 * i + 128].astype(F32)
+            g = gath[256 * u : 256 * u + 256, 128 * i : 128 * i + 128].astype(F32)
             total = total + g * g
-        sq_own[u] = jnp.broadcast_to(jnp.sum(total.T, axis=0, keepdims=True), (8, 128))
+        sq_own[u] = jnp.broadcast_to(jnp.sum(total.T, axis=0, keepdims=True), (8, 256))
         for j in (1, 3, 2):
             square_send(u, j).start()
-        p_own[u] = product(u, 0)
 
     def add(u):
         far_send(u, 0).wait_recv()
-        s_up[u, 0:64, :] = (p_up[u] + r_up[u].astype(F32)).astype(BF16)
+        s_up[u, 0:128, :] = (p_up[u] + r_up[u].astype(F32)).astype(BF16)
         late_send(u, 0).start()
         far_send(u, 1).wait_recv()
-        s_down[u, 64:128, :] = (p_down[u] + r_down[u].astype(F32)).astype(BF16)
+        s_down[u, 128:256, :] = (p_down[u] + r_down[u].astype(F32)).astype(BF16)
         late_send(u, 1).start()
 
     def finish(u):
-        for way in (0, 1):
-            early_send(u, way).wait_recv()
-            late_send(u, way).wait_recv()
         for j in (1, 2, 3):
             square_send(u, j).wait_recv()
         squares = sq_own[u] + sq_in[u, 0] + sq_in[u, 1] + sq_in[u, 2]
         scale = lax.rsqrt(squares / INNER + 1e-5)
-        scale = jnp.broadcast_to(scale[0:1], (128, 128)).T
+        scale = jnp.broadcast_to(scale[0:1], (128, 256)).T
+        for way in (0, 1):
+            early_send(u, way).wait_recv()
+            late_send(u, way).wait_recv()
         value = p_own[u] + f_up[u].astype(F32) + f_down[u].astype(F32)
         for half_of in (0, 128):
-            out_ref[128 * u : 128 * u + 128, half_of : half_of + 128] = (
+            out_ref[256 * u : 256 * u + 256, half_of : half_of + 128] = (
                 value[:, half_of : half_of + 128] * scale
             ).astype(BF16)
 
-    multiply(0)
-    multiply(1)
+    for u in range(4):
+        for way in (0, 1):
+            g_far(u, way, 2).wait_recv()
+        if u % 2 == 1:
+            multiply_far(u // 2)
+            multiply_near(u // 2)
+    square(0)
     add(0)
-    multiply(2)
+    p_own[0] = product(0, 0)
+    square(1)
     add(1)
-    multiply(3)
-    add(2)
-    finish(0)
-    lax.fori_loop(0, 16, drain_out, 0)
+    p_own[1] = product(1, 0)
+    drain_weights()
+    lax.fori_loop(0, 8, out_drain, 0)
+    out_own_drain()
     for d, k, hop in sent:
         t_send(d, k, hop).wait_send()
-    add(3)
-    for u in (1, 2, 3):
-        finish(u)
+    finish(0)
+    finish(1)
     for u in range(4):
         for way in (0, 1):
             g_near(u, way, 0).wait_send()
             g_far(u, way, -STEP[way]).wait_send()
+    for u in (0, 1):
+        for way in (0, 1):
             far_send(u, way).wait_send()
             early_send(u, way).wait_send()
             late_send(u, way).wait_send()
@@ -777,21 +876,21 @@
             pltpu.VMEM((4096, 256), BF16),
             pltpu.VMEM((4096, 256), BF16),
             pltpu.VMEM((80, 4096), BF16),
-            pltpu.VMEM((16, 128, 256), BF16),
+            pltpu.VMEM((128, 256), BF16),
             pltpu.VMEM((1024, 1024), BF16),
             pltpu.VMEM((TOK, 1024), BF16),
-            pltpu.VMEM((4, 8, 128), F32),
-            pltpu.VMEM((4, 3, 8, 128), F32),
-            pltpu.VMEM((4, 64, 256), F32),
-            pltpu.VMEM((4, 64, 256), F32),
-            pltpu.VMEM((4, 128, 256), F32),
-            pltpu.VMEM((4, 128, 256), BF16),
-            pltpu.VMEM((4, 128, 256), BF16),
-            pltpu.VMEM((4, 128, 256), BF16),
-            pltpu.VMEM((4, 64, 256), BF16),
-            pltpu.VMEM((4, 64, 256), BF16),
-            pltpu.VMEM((4, 128, 256), BF16),
-            pltpu.VMEM((4, 128, 256), BF16),
+            pltpu.VMEM((2, 8, 256), F32),
+            pltpu.VMEM((2, 3, 8, 256), F32),
+            pltpu.VMEM((2, 128, 256), F32),
+            pltpu.VMEM((2, 128, 256), F32),
+            pltpu.VMEM((2, 256, 256), F32),
+            pltpu.VMEM((2, 256, 256), BF16),
+            pltpu.VMEM((2, 256, 256), BF16),
+            pltpu.VMEM((2, 256, 256), BF16),
+            pltpu.VMEM((2, 128, 256), BF16),
+            pltpu.VMEM((2, 128, 256), BF16),
+            pltpu.VMEM((2, 256, 256), BF16),
+            pltpu.VMEM((2, 256, 256), BF16),
             pltpu.VMEM((HALO + TOK, 256), F32),
             pltpu.VMEM((TOK, 256), F32),
             pltpu.VMEM((HALO + TOK, 80), F32),
@@ -805,15 +904,16 @@
             pltpu.VMEM((128, 128), F32),
             dma((3,)),
             dma((2,)),
-            dma((7, 2, 9)),
-            dma((7, 2, 9)),
             dma((5, 2, 9)),
             dma((5, 2, 9)),
-            dma((2, 16)),
-            dma((2, 4, 4)),
-            dma((2, 4)),
-            dma((16,)),
-            dma((16,)),
+            dma((5, 2, 9)),
+            dma((5, 2, 9)),
+            dma((1,)),
+            dma((4,)),
+            dma((2, 2, 8)),
+            dma((2, 2, 8)),
+            dma((2, 3, 8)),
+            dma((2, 3, 8)),
             dma((3,)),
             dma((3,)),
             dma((4,)),
@@ -821,10 +921,10 @@
             dma((2, 9)),
             dma((4, 4)),
             dma((4, 4)),
-            dma((4, 3)),
-            dma((4, 3)),
-            dma((4, 3, 2)),
-            dma((4, 3, 2)),
+            dma((2, 3)),
+            dma((2, 3)),
+            dma((2, 3, 2)),
+            dma((2, 3, 2)),
         ],
         compiler_params=pltpu.CompilerParams(
             collective_id=0, has_side_effects=True, vmem_limit_bytes=67043328

time: 115 us -> 109 us (0.948)
  the two profiles are of different devices: /device:TPU:36 before, /device:TPU:1 now
where the time goes in v3:
time: 109 us; the launch traced here: 108 us
  Pallas kernels  107 us (98%)
  local copies, waits for them, and re-layouts  1.67 us (2%)
    pallas_call x1, Pallas kernels, local(): pl.pallas_call(kernel, out_shape=jax.ShapeDtypeStruct((TOK, 256), BF16),...  107 us

profile of v3, /device:TPU:1, one launch (start us, length us, event | category | flops | bytes accessed | tf_op | source)
XLA Modules:
  0.0 108.4 jit_solution(14798265464555919126)
XLA Ops:
  0.0 106.7 %shard_map.118 = bf16[512,256]{1,0:T(8,128)(2,1)} custom-call(bf16[512,4096]{1,0:T(8,128)(2,1)} %act_hbm.1, bf16[128,256]{1,0:T(8,128)(2,1)} %wi_hbm.1, bf16[128,256]{1,0:T(8,128)(2,1)} %wg_hbm.1, bf16[128,256]{1,0:T(8,128)(2,1)} %wo_hbm.1, bf16[128,1024]{1,0:T(8,128)(2,1)} %wgr_hbm.1, bf16[64,128]{1,0:T(8,128)(2,1)} %bitcast.2, f32[4,256]{1,0:T(4,128)} %tapi_hbm.1, ...), custom_call_target="tpu_custom_call" | custom-call | tf_op jit(solution)/shard_map/pallas_call | solution.py:859
  106.7 1.7 %copy.14 = bf16[512,256]{1,0:T(8,128)(2,1)} copy(bf16[512,256]{1,0:T(8,128)(2,1)} %shard_map.118) | data formatting | bytes 524288

commit v4 on v3

--- a/solution.py
+++ b/solution.py
@@ -13,6 +13,7 @@
 HALO = 8
 NZ = 16
 FAR = ((8, 7), (8, 7), (7, 8), (8, 7), (7, 8))
+KIND = (0, 1, 1, 2, 2)
 
 
 def remote(src, dst, send, recv, device):
@@ -86,6 +87,7 @@
     zr,
     bs,
     br,
+    br_gate,
     cs,
     cr,
     os_,
@@ -184,6 +186,12 @@
         after,
     )
 
+    def sent_all(sem, ref):
+        remote(ref, ref, sem, sem, sib).wait_send()
+
+    def got_all(sem, ref):
+        remote(ref, ref, sem, sem, sib).wait_recv()
+
     def block(p, zz):
         row = pl.multiple_of((2 * zz + c) * 128, 128)
         if p == 0:
@@ -193,14 +201,11 @@
             return w_in.at[pl.ds(row + part, 64), :]
         return w_gate.at[pl.ds(row + part, 64), :]
 
-    def sib_block(p, zz):
+    def sib_block(kind, zz):
         row = pl.multiple_of((2 * zz + 1 - c) * 128, 128)
-        if p == 0:
+        if kind == 0:
             return w_gs.at[:, pl.ds(row, 128)]
-        part = 64 * ((p - 1) % 2)
-        if p < 3:
-            return w_in.at[pl.ds(row + part, 64), :]
-        return w_gate.at[pl.ds(row + part, 64), :]
+        return w_in.at[pl.ds(row, 128), :]
 
     def origin(d, k):
         return zmod(z - k) if d == 0 else zmod(z + k)
@@ -208,15 +213,16 @@
     def ring(p, d, k, recv_k):
         ref = block(p, origin(d, k))
         target = zmod(z + 1) if d == 0 else zmod(z - 1)
-        return remote(ref, ref, zs.at[p, d, k], zr.at[p, d, recv_k], dev(target, c, h))
+        return remote(ref, ref, zs.at[KIND[p]], zr.at[p, d, recv_k - 1], dev(target, c, h))
 
     def to_sib(p, d, k):
         ref = block(p, origin(d, k))
-        return remote(ref, ref, bs.at[p, d, k], br.at[p, d, k], sib)
-
-    def from_sib(p, d, k):
-        ref = sib_block(p, origin(d, k))
-        remote(ref, ref, bs.at[p, d, k], br.at[p, d, k], sib).wait_recv()
+        kind = KIND[p]
+        landed = br_gate.at[0] if kind == 2 else br.at[kind, 0 if k == 8 else d, k]
+        return remote(ref, ref, bs.at[kind], landed, sib)
+
+    def from_sib(kind, d, k):
+        got_all(br.at[kind, d, k], sib_block(kind, origin(d, k)))
 
     keeper = z % 4
     is_source = keeper == y
@@ -234,7 +240,7 @@
             land,
             w_out.at[pl.ds(out_rows(z, c), 128), pl.ds(pl.multiple_of(256 * column, 256), 256)],
             cs.at[0],
-            cr.at[column],
+            cr.at[0],
             dev(z, c, x * 4 + keeper),
         )
 
@@ -250,11 +256,11 @@
     def out_send(a, d, zz, column, slot):
         ref = out_part(a, zz, c, column)
         target = zmod(z + 1) if d == 0 else zmod(z - 1)
-        return remote(ref, ref, os_.at[a, d, slot], orr.at[a, d, slot], dev(target, c, h))
+        return remote(ref, ref, os_.at[d], orr.at[a, d, slot], dev(target, c, h))
 
     def out_to_sib(a, d, zz, column, slot):
         ref = out_part(a, zz, c, column)
-        return remote(ref, ref, ws.at[a, d, slot], wr.at[a, d, slot], sib)
+        return remote(ref, ref, ws.at[0], wr.at[0], sib)
 
     def next_slot(d, q):
         return jnp.where(near[d] < 4, q, q + 4)
@@ -264,8 +270,7 @@
 
             @pl.when(is_source)
             def _():
-                for step in (1, 2, 3):
-                    bring(lax.rem(y + step, 4)).wait_recv()
+                got_all(cr.at[0], w_out.at[pl.ds(0, 96), :])
 
         if t < 4:
 
@@ -293,56 +298,25 @@
 
                         out_to_sib(a, d, zz, column, q).start()
 
-    def out_end(q, carry):
-        for a in (0, 1):
-            for d in (0, 1):
-                reach = out_dist(d, q)
-
-                @pl.when(reach <= OUT_FAR[a][d])
-                def _():
-                    zz, column = out_origin(d, q), q % 4
-                    theirs = out_part(a, zz, 1 - c, column)
-                    remote(theirs, theirs, ws.at[a, d, q], wr.at[a, d, q], sib).wait_recv()
-
-        return carry
-
-    def out_own_end():
-        @pl.when(is_source)
-        def _():
-            for a in (0, 1):
-                for column in range(4):
-                    theirs = out_part(a, z, 1 - c, column)
-                    remote(theirs, theirs, ws.at[a, 2, column], wr.at[a, 2, column], sib).wait_recv()
-
-    def out_drain(q, carry):
-        for a in (0, 1):
-            for d in (0, 1):
-                reach = out_dist(d, q)
-
-                @pl.when(reach <= OUT_FAR[a][d])
-                def _():
-                    zz, column = out_origin(d, q), q % 4
-
-                    @pl.when(reach < OUT_FAR[a][d])
-                    def _():
-                        out_send(a, d, zz, column, next_slot(d, q)).wait_send()
-
-                    out_to_sib(a, d, zz, column, q).wait_send()
-
-        return carry
-
-    def out_own_drain():
-        @pl.when(is_source)
-        def _():
-            for a in (0, 1):
-                for column in range(4):
-                    for d in (0, 1):
-                        out_send(a, d, z, column, column).wait_send()
-                    out_to_sib(a, 2, z, column, column).wait_send()
+    def out_end():
+        got_all(wr.at[0], w_out.at[pl.ds(0, 512), :])
+
+    def out_drain():
+        for d in (0, 1):
+
+            @pl.when(near[d] == 3)
+            def _():
+                sent_all(os_.at[d], w_out.at[pl.ds(0, 192), :])
+
+            @pl.when(near[d] != 3)
+            def _():
+                sent_all(os_.at[d], w_out.at[pl.ds(0, 256), :])
+
+        sent_all(ws.at[0], w_out.at[pl.ds(0, 512), :])
 
         @pl.when(jnp.logical_not(is_source))
         def _():
-            bring(y).wait_send()
+            sent_all(cs.at[0], land)
 
     def hand_on(p, d, k):
         to_sib(p, d, k).start()
@@ -378,12 +352,6 @@
             for zz in planes
         )
 
-    def gate_dots(*planes):
-        acc_g[...] += sum(
-            jnp.dot(act[HALO:, columns(zz)], w_gate[columns(zz), :], preferred_element_type=F32)
-            for zz in planes
-        )
-
     first(0)
     load_in.wait()
     first(1)
@@ -391,6 +359,7 @@
     send_halo.start()
     load_gate.wait()
     first(3)
+    first(4)
     scaled = (wo_ref[...].astype(F32) * gain_ref[...]).astype(BF16)
 
     @pl.when(is_source)
@@ -404,7 +373,6 @@
 
     acc_i[...] = jnp.zeros_like(acc_i)
     acc_s[...] = jnp.zeros_like(acc_s)
-    acc_g[...] = jnp.zeros_like(acc_g)
 
     def serve(pieces, k):
         for p in pieces:
@@ -412,15 +380,13 @@
                 if k <= FAR[p][d]:
                     event(p, d, k, k < FAR[p][d])
 
-    def use(pieces, dots, k):
-        for p in pieces:
-            for d in (0, 1):
-                if k <= FAR[p][d]:
-                    from_sib(p, d, k)
-        if k < 8:
+    def use(kind, dots, k):
+        from_sib(kind, 0, k)
+        if k == 8:
+            dots(origin(0, k))
+        else:
+            from_sib(kind, 1, k)
             dots(origin(0, k), origin(1, k))
-        else:
-            dots(origin(0, k))
 
     IN = (1, 2)
     GATE = (3, 4)
@@ -429,21 +395,21 @@
     serve(IN, 1)
     load_act.wait()
     send_halo.wait()
-    for p in (0, 1, 2):
-        from_sib(p, 0, 0)
+    for kind in (0, 1):
+        from_sib(kind, 0, 0)
     dots_gs(z)
     dots_in(z)
     for k in (2, 3, 4, 5, 6, 7):
         serve((0, 1), k)
-        use((0,), dots_gs, k - 1)
+        use(0, dots_gs, k - 1)
         serve((2,), k)
-        use(IN, dots_in, k - 1)
-        serve((3,), k - 1)
+        use(1, dots_in, k - 1)
+        serve(GATE, k - 1)
+    serve_out(0)
     serve((0,), 8)
-    first(4)
-    serve_out(0)
-    use((0,), dots_gs, 7)
-    use((0,), dots_gs, 8)
+    use(0, dots_gs, 7)
+    use(0, dots_gs, 8)
+    serve_out(1)
 
     not_first = jnp.where(s == 0, 0.0, 1.0).astype(F32)
     lane128 = lax.broadcasted_iota(jnp.int32, (TOK, 128), 1)
@@ -463,14 +429,14 @@
 
     def y_copy(j, where):
         rows = bct.at[pl.ds(pl.multiple_of(64 * where, 64), 64), :]
-        return remote(rows, rows, ys.at[j - 1], yr.at[j - 1], dev(z, c, hid_at(0, j)))
+        return remote(rows, rows, ys.at[0], yr.at[0], dev(z, c, hid_at(0, j)))
 
     for j in (1, 3, 2):
         y_copy(j, y).start()
 
     serve(IN, 8)
-    serve((3,), 7)
-    use(IN, dots_in, 7)
+    serve(GATE, 7)
+    use(1, dots_in, 7)
 
     step4 = jnp.where(
         y < 2,
@@ -504,10 +470,8 @@
             halves.append(jnp.where(lane128 < 64, lo, hi))
         return jnp.concatenate(halves, axis=1)
 
-    use(IN, dots_in, 8)
-    serve((3,), 8)
-    serve((4,), 1)
-    serve_out(1)
+    use(1, dots_in, 8)
+    serve_out(2)
     acc_i[...] = acc_i[...].astype(BF16).astype(F32)
     acc_i[0:HALO, :] = acc_i[0:HALO, :] * not_first
     conv = jnp.zeros((TOK, 256), F32)
@@ -522,9 +486,8 @@
     decay0 = expcum[255:256]
     decay1 = expcum[511:512]
 
-    for j in (1, 2, 3):
-        y_copy(j, lax.rem(y + 4 - j, 4)).wait()
-
+    serve_out(3)
+    got_all(yr.at[0], bct.at[pl.ds(0, 192), :])
     fresh0 = jnp.dot(bct[0:128, 0:256], weighted[0:256], preferred_element_type=F32)
     fresh1 = jnp.dot(bct[0:128, 256:512], weighted[256:512], preferred_element_type=F32)
     end_own = decay1 * fresh0 + fresh1
@@ -536,8 +499,7 @@
     swap = remote(e_own, e_sib, es.at[0], es.at[1], sib)
     swap.start()
 
-    serve((4,), 2)
-    serve_out(2)
+    serve(GATE, 8)
     swap.wait()
 
     end_sib = e_sib[0:128, :].astype(F32)
@@ -558,21 +520,20 @@
     def t_send(d, k, hop):
         ref = tbuf.at[origin(d, k)]
         target = zmod(z + hop) if d == 0 else zmod(z - hop)
-        return remote(ref, ref, ts.at[hop - 1, d, k], tr.at[d, k + hop], dev(target, c, h))
+        return remote(ref, ref, ts.at[0], tr.at[d, k + hop - 1], dev(target, c, h))
 
     def t_recv(d, k):
         ref = tbuf.at[origin(d, k)]
-        remote(ref, ref, ts.at[0, d, k], tr.at[d, k], sib).wait_recv()
-
-    sent = []
+        got_all(tr.at[d, k - 1], ref)
 
     def t_start(d, k, hop):
         t_send(d, k, hop).start()
-        sent.append((d, k, hop))
 
     for hop in (2, 1):
         for d in (0, 1):
             t_start(d, 0, hop)
+
+    serve_out(4)
 
     row = lax.broadcasted_iota(jnp.int32, (256, 256), 0)
     column = lax.broadcasted_iota(jnp.int32, (256, 256), 1)
@@ -592,15 +553,22 @@
         return total
 
     mixed0 = span(0)
-    serve((4,), 3)
-    serve_out(3)
+
+    def gate_half(q):
+        tokens = slice(256 * q, 256 * q + 256)
+        acc_g[tokens, :] = jnp.dot(
+            act[HALO + 256 * q : HALO + 256 * q + 256, :], w_gate[...], preferred_element_type=F32
+        )
+
+    got_all(br_gate.at[0], w_gate.at[pl.ds(0, 2048), :])
+    gate_half(0)
     for d in (0, 1):
         t_recv(d, 2)
         for hop in (2, 1):
             t_start(d, 2, hop)
-    serve((4,), 4)
+    serve_out(5)
     mixed1 = span(1)
-    serve_out(4)
+    gate_half(1)
     skip = jnp.where(
         head_lane < 2,
         jnp.where(head_lane == 0, skip_ref[0], skip_ref[1]),
@@ -613,24 +581,13 @@
         t_recv(d, 4)
         for hop in (2, 1):
             t_start(d, 4, hop)
-    serve((4,), 5)
-    serve_out(5)
-    for p in GATE:
-        from_sib(p, 0, 0)
-    gate_dots(z)
-    for k in (1, 2, 3, 4):
-        use(GATE, gate_dots, k)
+    serve_out(6)
     t_recv(0, 6)
     for hop in (2, 1):
         t_start(0, 6, hop)
     t_recv(1, 6)
     t_start(1, 6, 1)
-    serve((4,), 6)
-    serve_out(6)
-    use(GATE, gate_dots, 5)
-    serve((4,), 7)
     serve_out(7)
-    use(GATE, gate_dots, 6)
     for d, ks in ((0, (1, 3, 5, 7, 8)), (1, (1, 3, 5, 7))):
         for k in ks:
             t_recv(d, k)
@@ -644,9 +601,7 @@
     pbuf[...] = prefix
     swap2 = remote(pbuf, psib, es.at[2], es.at[3], sib)
     swap2.start()
-    serve((4,), 8)
-    use(GATE, gate_dots, 7)
-    use(GATE, gate_dots, 8)
+    serve_out(8)
     swap2.wait()
     other = psib[...]
     before = jnp.where(
@@ -676,12 +631,12 @@
 
     def g_near(u, way, a):
         ref = part(u, a, 0, 128)
-        return remote(ref, ref, gs.at[u, way], gr.at[u, way], dev(z, c, hid_at(0, STEP[way])))
+        return remote(ref, ref, gs.at[0], gr.at[u, way], dev(z, c, hid_at(0, STEP[way])))
 
     def g_far(u, way, a):
         ref = part(u, a, 64 * way, 64)
         return remote(
-            ref, ref, gs.at[u, 2 + way], gr.at[u, 2 + way], dev(z, c, hid_at(0, STEP[way]))
+            ref, ref, gs.at[0], gr.at[u, 2], dev(z, c, hid_at(0, STEP[way]))
         )
 
     def near_start(u):
@@ -698,34 +653,23 @@
     near_start(1)
     gated(1, mixed1, state1)
     near_start(2)
-    serve_out(8)
+    serve_out(9)
 
     def drain_weights():
-        for p in range(5):
-            for d in (0, 1):
-
-                def drain(k, carry):
-                    ring(p, d, k, k + 1).wait_send()
-                    return carry
-
-                lax.fori_loop(0, FAR[p][d], drain, 0)
-
-                def drain_sib(k, carry):
-                    to_sib(p, d, k).wait_send()
-                    return carry
-
-                lax.fori_loop(d, FAR[p][d] + 1, drain_sib, 0)
+        sent_all(zs.at[0], w_gs.at[:, pl.ds(0, 1920)])
+        sent_all(bs.at[0], w_gs.at[:, pl.ds(0, 2048)])
+        for kind, ref in ((1, w_in), (2, w_gate)):
+            sent_all(zs.at[kind], ref.at[pl.ds(0, 1920), :])
+            sent_all(bs.at[kind], ref.at[pl.ds(0, 2048), :])
 
     near_take(0)
     near_take(1)
     near_start(3)
-    serve_out(9)
+    serve_out(10)
     near_take(2)
-    serve_out(10)
+    serve_out(11)
     near_take(3)
-    serve_out(11)
-    lax.fori_loop(0, 8, out_end, 0)
-    out_own_end()
+    out_end()
 
     def product(u, offset):
         rows = pl.ds(pl.multiple_of(256 * lax.rem(x + offset, 4), 256), 256)
@@ -737,9 +681,8 @@
         )
 
     def along(u, slot, way, src, dst):
-        return remote(
-            src, dst, hs.at[u, slot, way], hr.at[u, slot, way], dev(z, c, hid_at(STEP[way], 0))
-        )
+        landed = hr.at[u, way if slot == 0 else 2]
+        return remote(src, dst, hs.at[0], landed, dev(z, c, hid_at(STEP[way], 0)))
 
     top = pl.ds(0, 128)
     low = pl.ds(128, 128)
@@ -757,7 +700,7 @@
 
     def square_send(u, j):
         return remote(
-            sq_own.at[u], sq_in.at[u, j - 1], qs.at[u, j - 1], qr.at[u, j - 1], dev(z, c, hid_at(j, 0))
+            sq_own.at[u], sq_in.at[u, j - 1], qs.at[0], qr.at[u], dev(z, c, hid_at(j, 0))
         )
 
     def multiply_far(u):
@@ -793,14 +736,11 @@
         late_send(u, 1).start()
 
     def finish(u):
-        for j in (1, 2, 3):
-            square_send(u, j).wait_recv()
+        got_all(qr.at[u], sq_in.at[u])
         squares = sq_own[u] + sq_in[u, 0] + sq_in[u, 1] + sq_in[u, 2]
         scale = lax.rsqrt(squares / INNER + 1e-5)
         scale = jnp.broadcast_to(scale[0:1], (128, 256)).T
-        for way in (0, 1):
-            early_send(u, way).wait_recv()
-            late_send(u, way).wait_recv()
+        got_all(hr.at[u, 2], gath.at[pl.ds(0, 128), :])
         value = p_own[u] + f_up[u].astype(F32) + f_down[u].astype(F32)
         for half_of in (0, 128):
             out_ref[256 * u : 256 * u + 256, half_of : half_of + 128] = (
@@ -808,8 +748,7 @@
             ).astype(BF16)
 
     for u in range(4):
-        for way in (0, 1):
-            g_far(u, way, 2).wait_recv()
+        got_all(gr.at[u, 2], part(u, 2, 0, 128))
         if u % 2 == 1:
             multiply_far(u // 2)
             multiply_near(u // 2)
@@ -820,23 +759,14 @@
     add(1)
     p_own[1] = product(1, 0)
     drain_weights()
-    lax.fori_loop(0, 8, out_drain, 0)
-    out_own_drain()
-    for d, k, hop in sent:
-        t_send(d, k, hop).wait_send()
+    out_drain()
+    sent_all(ys.at[0], bct.at[pl.ds(0, 192), :])
+    sent_all(ts.at[0], tbuf.at[pl.ds(0, 15)])
     finish(0)
     finish(1)
-    for u in range(4):
-        for way in (0, 1):
-            g_near(u, way, 0).wait_send()
-            g_far(u, way, -STEP[way]).wait_send()
-    for u in (0, 1):
-        for way in (0, 1):
-            far_send(u, way).wait_send()
-            early_send(u, way).wait_send()
-            late_send(u, way).wait_send()
-        for j in (1, 2, 3):
-            square_send(u, j).wait_send()
+    sent_all(gs.at[0], gath.at[pl.ds(0, 384), :])
+    sent_all(hs.at[0], gath.at[pl.ds(0, 384), :])
+    sent_all(qs.at[0], sq_in)
 
 
 def local(
@@ -904,27 +834,28 @@
             pltpu.VMEM((128, 128), F32),
             dma((3,)),
             dma((2,)),
-            dma((5, 2, 9)),
-            dma((5, 2, 9)),
-            dma((5, 2, 9)),
-            dma((5, 2, 9)),
+            dma((3,)),
+            dma((5, 2, 8)),
+            dma((3,)),
+            dma((2, 2, 9)),
+            dma((1,)),
+            dma((1,)),
+            dma((1,)),
+            dma((2,)),
+            dma((2, 2, 8)),
+            dma((1,)),
+            dma((1,)),
+            dma((1,)),
             dma((1,)),
             dma((4,)),
-            dma((2, 2, 8)),
-            dma((2, 2, 8)),
-            dma((2, 3, 8)),
-            dma((2, 3, 8)),
-            dma((3,)),
-            dma((3,)),
-            dma((4,)),
-            dma((2, 2, 9)),
-            dma((2, 9)),
-            dma((4, 4)),
-            dma((4, 4)),
+            dma((1,)),
+            dma((2, 8)),
+            dma((1,)),
+            dma((4, 3)),
+            dma((1,)),
+            dma((2,)),
+            dma((1,)),
             dma((2, 3)),
-            dma((2, 3)),
-            dma((2, 3, 2)),
-            dma((2, 3, 2)),
         ],
         compiler_params=pltpu.CompilerParams(
             collective_id=0, has_side_effects=True, vmem_limit_bytes=67043328

time: 109 us -> 98.9 us (0.907)
  Pallas kernels: 107 us -> 97.1 us
    pallas_call x1, Pallas kernels: 107 us -> 97.1 us  [local(): pl.pallas_call(kernel, out_shape=jax.ShapeDtypeStruct((TOK, 256), BF16),...]
where the time goes in v4:
time: 98.9 us; the launch traced here: 98.8 us
  Pallas kernels  97.1 us (98%)
  local copies, waits for them, and re-layouts  1.67 us (2%)
    pallas_call x1, Pallas kernels, local(): pl.pallas_call(kernel, out_shape=jax.ShapeDtypeStruct((TOK, 256), BF16),...  97.1 us

profile of v4, /device:TPU:1, one launch (start us, length us, event | category | flops | bytes accessed | tf_op | source)
XLA Modules:
  0.0 98.8 jit_solution(8295376168083288951)
XLA Ops:
  0.0 97.1 %shard_map.118 = bf16[512,256]{1,0:T(8,128)(2,1)} custom-call(bf16[512,4096]{1,0:T(8,128)(2,1)} %act_hbm.1, bf16[128,256]{1,0:T(8,128)(2,1)} %wi_hbm.1, bf16[128,256]{1,0:T(8,128)(2,1)} %wg_hbm.1, bf16[128,256]{1,0:T(8,128)(2,1)} %wo_hbm.1, bf16[128,1024]{1,0:T(8,128)(2,1)} %wgr_hbm.1, bf16[64,128]{1,0:T(8,128)(2,1)} %bitcast.2, f32[4,256]{1,0:T(4,128)} %tapi_hbm.1, ...), custom_call_target="tpu_custom_call" | custom-call | tf_op jit(solution)/shard_map/pallas_call | solution.py:789
  97.1 1.7 %copy.14 = bf16[512,256]{1,0:T(8,128)(2,1)} copy(bf16[512,256]{1,0:T(8,128)(2,1)} %shard_map.118) | data formatting | bytes 524288

commit v5 on v4

--- a/solution.py
+++ b/solution.py
@@ -403,8 +403,9 @@
         serve((0, 1), k)
         use(0, dots_gs, k - 1)
         serve((2,), k)
+        serve((3,), k - 1)
         use(1, dots_in, k - 1)
-        serve(GATE, k - 1)
+        serve((4,), k - 1)
     serve_out(0)
     serve((0,), 8)
     use(0, dots_gs, 7)
@@ -434,10 +435,6 @@
     for j in (1, 3, 2):
         y_copy(j, y).start()
 
-    serve(IN, 8)
-    serve(GATE, 7)
-    use(1, dots_in, 7)
-
     step4 = jnp.where(
         y < 2,
         jnp.where(y == 0, both_t[64:68], both_t[68:72]),
@@ -470,6 +467,9 @@
             halves.append(jnp.where(lane128 < 64, lo, hi))
         return jnp.concatenate(halves, axis=1)
 
+    serve(IN, 8)
+    serve(GATE, 7)
+    use(1, dots_in, 7)
     use(1, dots_in, 8)
     serve_out(2)
     acc_i[...] = acc_i[...].astype(BF16).astype(F32)
@@ -671,10 +671,13 @@
     near_take(3)
     out_end()
 
+    SPLIT = ((0, 256), (256, 128), (384, 128))
+
     def product(u, offset):
+        start, count = SPLIT[u]
         rows = pl.ds(pl.multiple_of(256 * lax.rem(x + offset, 4), 256), 256)
         return lax.dot_general(
-            gath[256 * u : 256 * u + 256, :],
+            gath[start : start + count, :],
             w_out[rows, :],
             (((1,), (1,)), ((), ())),
             preferred_element_type=F32,
@@ -684,86 +687,115 @@
         landed = hr.at[u, way if slot == 0 else 2]
         return remote(src, dst, hs.at[0], landed, dev(z, c, hid_at(STEP[way], 0)))
 
-    top = pl.ds(0, 128)
-    low = pl.ds(128, 128)
+    def halves(u):
+        start, count = SPLIT[u]
+        half = count // 2
+        return pl.ds(start, half), pl.ds(start + half, half), pl.ds(start // 2, half)
 
     def far_send(u, way):
-        return along(u, 0, way, s_far.at[u, (top, low)[way]], (r_up, r_down)[way].at[u])
+        rows = halves(u)
+        return along(u, 0, way, s_far.at[rows[way]], (r_up, r_down)[way].at[rows[2]])
 
     def early_send(u, way):
-        rows = (low, top)[way]
-        return along(u, 1, way, (s_up, s_down)[way].at[u, rows], (f_up, f_down)[way].at[u, rows])
+        rows = halves(u)[1 - way]
+        return along(u, 1, way, (s_up, s_down)[way].at[rows], (f_up, f_down)[way].at[rows])
 
     def late_send(u, way):
-        rows = (top, low)[way]
-        return along(u, 2, way, (s_up, s_down)[way].at[u, rows], (f_up, f_down)[way].at[u, rows])
+        rows = halves(u)[way]
+        return along(u, 2, way, (s_up, s_down)[way].at[rows], (f_up, f_down)[way].at[rows])
 
     def square_send(u, j):
+        start, count = SPLIT[u]
+        lanes = pl.ds(start, count)
         return remote(
-            sq_own.at[u], sq_in.at[u, j - 1], qs.at[0], qr.at[u], dev(z, c, hid_at(j, 0))
+            sq_own.at[:, lanes], sq_in.at[j - 1, :, lanes], qs.at[0], qr.at[u], dev(z, c, hid_at(j, 0))
         )
 
     def multiply_far(u):
-        s_far[u] = product(u, 2).astype(BF16)
+        start, count = SPLIT[u]
+        s_far[start : start + count, :] = product(u, 2).astype(BF16)
         for way in (0, 1):
             far_send(u, way).start()
 
     def multiply_near(u):
+        top, low, kept = halves(u)
+        half = SPLIT[u][1] // 2
         up = product(u, 1)
-        s_up[u, 128:256, :] = up[128:256].astype(BF16)
+        s_up[low, :] = up[half:].astype(BF16)
         early_send(u, 0).start()
-        p_up[u] = up[0:128]
+        p_up[kept, :] = up[:half]
         down = product(u, 3)
-        s_down[u, 0:128, :] = down[0:128].astype(BF16)
+        s_down[top, :] = down[:half].astype(BF16)
         early_send(u, 1).start()
-        p_down[u] = down[128:256]
+        p_down[kept, :] = down[half:]
 
     def square(u):
-        total = jnp.zeros((256, 128), F32)
+        start, count = SPLIT[u]
+        total = jnp.zeros((count, 128), F32)
         for i in range(8):
-            g = gath[256 * u : 256 * u + 256, 128 * i : 128 * i + 128].astype(F32)
+            g = gath[start : start + count, 128 * i : 128 * i + 128].astype(F32)
             total = total + g * g
-        sq_own[u] = jnp.broadcast_to(jnp.sum(total.T, axis=0, keepdims=True), (8, 256))
+        sq_own[:, start : start + count] = jnp.broadcast_to(
+            jnp.sum(total.T, axis=0, keepdims=True), (8, count)
+        )
         for j in (1, 3, 2):
             square_send(u, j).start()
 
     def add(u):
+        top, low, kept = halves(u)
         far_send(u, 0).wait_recv()
-        s_up[u, 0:128, :] = (p_up[u] + r_up[u].astype(F32)).astype(BF16)
+        s_up[top, :] = (p_up[kept, :] + r_up[kept, :].astype(F32)).astype(BF16)
         late_send(u, 0).start()
         far_send(u, 1).wait_recv()
-        s_down[u, 128:256, :] = (p_down[u] + r_down[u].astype(F32)).astype(BF16)
+        s_down[low, :] = (p_down[kept, :] + r_down[kept, :].astype(F32)).astype(BF16)
         late_send(u, 1).start()
 
+    def own(u):
+        start, count = SPLIT[u]
+        p_own[start : start + count, :] = product(u, 0)
+
     def finish(u):
-        got_all(qr.at[u], sq_in.at[u])
-        squares = sq_own[u] + sq_in[u, 0] + sq_in[u, 1] + sq_in[u, 2]
+        start, count = SPLIT[u]
+        tokens = slice(start, start + count)
+        got_all(qr.at[u], sq_in.at[:, :, pl.ds(start, count)])
+        squares = sq_own[:, tokens] + sq_in[0, :, tokens] + sq_in[1, :, tokens] + sq_in[2, :, tokens]
         scale = lax.rsqrt(squares / INNER + 1e-5)
-        scale = jnp.broadcast_to(scale[0:1], (128, 256)).T
-        got_all(hr.at[u, 2], gath.at[pl.ds(0, 128), :])
-        value = p_own[u] + f_up[u].astype(F32) + f_down[u].astype(F32)
+        scale = jnp.broadcast_to(scale[0:1], (128, count)).T
+        got_all(hr.at[u, 2], gath.at[pl.ds(0, count // 2), :])
+        value = p_own[tokens, :] + f_up[tokens, :].astype(F32) + f_down[tokens, :].astype(F32)
         for half_of in (0, 128):
-            out_ref[256 * u : 256 * u + 256, half_of : half_of + 128] = (
+            out_ref[tokens, half_of : half_of + 128] = (
                 value[:, half_of : half_of + 128] * scale
             ).astype(BF16)
 
-    for u in range(4):
+    def far_take(u):
         got_all(gr.at[u, 2], part(u, 2, 0, 128))
-        if u % 2 == 1:
-            multiply_far(u // 2)
-            multiply_near(u // 2)
+
+    far_take(0)
+    far_take(1)
+    multiply_far(0)
+    multiply_near(0)
+    far_take(2)
+    multiply_far(1)
+    multiply_near(1)
+    far_take(3)
+    multiply_far(2)
+    multiply_near(2)
+    add(0)
     square(0)
-    add(0)
-    p_own[0] = product(0, 0)
     square(1)
     add(1)
-    p_own[1] = product(1, 0)
+    square(2)
+    own(0)
+    add(2)
+    own(1)
+    own(2)
     drain_weights()
     out_drain()
     sent_all(ys.at[0], bct.at[pl.ds(0, 192), :])
     sent_all(ts.at[0], tbuf.at[pl.ds(0, 15)])
-    finish(0)
-    finish(1)
+    for u in (0, 1, 2):
+        finish(u)
     sent_all(gs.at[0], gath.at[pl.ds(0, 384), :])
     sent_all(hs.at[0], gath.at[pl.ds(0, 384), :])
     sent_all(qs.at[0], sq_in)
@@ -809,18 +841,18 @@
             pltpu.VMEM((128, 256), BF16),
             pltpu.VMEM((1024, 1024), BF16),
             pltpu.VMEM((TOK, 1024), BF16),
-            pltpu.VMEM((2, 8, 256), F32),
-            pltpu.VMEM((2, 3, 8, 256), F32),
-            pltpu.VMEM((2, 128, 256), F32),
-            pltpu.VMEM((2, 128, 256), F32),
-            pltpu.VMEM((2, 256, 256), F32),
-            pltpu.VMEM((2, 256, 256), BF16),
-            pltpu.VMEM((2, 256, 256), BF16),
-            pltpu.VMEM((2, 256, 256), BF16),
-            pltpu.VMEM((2, 128, 256), BF16),
-            pltpu.VMEM((2, 128, 256), BF16),
-            pltpu.VMEM((2, 256, 256), BF16),
-            pltpu.VMEM((2, 256, 256), BF16),
+            pltpu.VMEM((8, TOK), F32),
+            pltpu.VMEM((3, 8, TOK), F32),
+            pltpu.VMEM((256, 256), F32),
+            pltpu.VMEM((256, 256), F32),
+            pltpu.VMEM((TOK, 256), F32),
+            pltpu.VMEM((TOK, 256), BF16),
+            pltpu.VMEM((TOK, 256), BF16),
+            pltpu.VMEM((TOK, 256), BF16),
+            pltpu.VMEM((256, 256), BF16),
+            pltpu.VMEM((256, 256), BF16),
+            pltpu.VMEM((TOK, 256), BF16),
+            pltpu.VMEM((TOK, 256), BF16),
             pltpu.VMEM((HALO + TOK, 256), F32),
             pltpu.VMEM((TOK, 256), F32),
             pltpu.VMEM((HALO + TOK, 80), F32),
@@ -853,9 +885,9 @@
             dma((1,)),
             dma((4, 3)),
             dma((1,)),
-            dma((2,)),
-            dma((1,)),
-            dma((2, 3)),
+            dma((3,)),
+            dma((1,)),
+            dma((3, 3)),
         ],
         compiler_params=pltpu.CompilerParams(
             collective_id=0, has_side_effects=True, vmem_limit_bytes=67043328

time: 98.9 us -> 98.5 us (level)
  no operation moved by 1% of the time
where the time goes in v5:
time: 98.5 us; the launch traced here: 98.3 us
  Pallas kernels  96.7 us (98%)
  local copies, waits for them, and re-layouts  1.67 us (2%)
    pallas_call x1, Pallas kernels, local(): pl.pallas_call(kernel, out_shape=jax.ShapeDtypeStruct((TOK, 256), BF16),...  96.7 us

profile of v5, /device:TPU:1, one launch (start us, length us, event | category | flops | bytes accessed | tf_op | source)
XLA Modules:
  0.0 98.3 jit_solution(163319665049908222)
XLA Ops:
  0.0 96.7 %shard_map.118 = bf16[512,256]{1,0:T(8,128)(2,1)} custom-call(bf16[512,4096]{1,0:T(8,128)(2,1)} %act_hbm.1, bf16[128,256]{1,0:T(8,128)(2,1)} %wi_hbm.1, bf16[128,256]{1,0:T(8,128)(2,1)} %wg_hbm.1, bf16[128,256]{1,0:T(8,128)(2,1)} %wo_hbm.1, bf16[128,1024]{1,0:T(8,128)(2,1)} %wgr_hbm.1, bf16[64,128]{1,0:T(8,128)(2,1)} %bitcast.2, f32[4,256]{1,0:T(4,128)} %tapi_hbm.1, ...), custom_call_target="tpu_custom_call" | custom-call | tf_op jit(solution)/shard_map/pallas_call | solution.py:821
  96.7 1.7 %copy.14 = bf16[512,256]{1,0:T(8,128)(2,1)} copy(bf16[512,256]{1,0:T(8,128)(2,1)} %shard_map.118) | data formatting | bytes 524288

commit v6 on v5

--- a/solution.py
+++ b/solution.py
@@ -126,6 +126,15 @@
     after = {"seq": lax.rem(s + 1, 32), "hid": h}
     extra = {"seq": lax.rem(s + 2 * c - 1 + 32, 32), "hid": h}
 
+    barrier = pltpu.get_barrier_semaphore()
+    for step in (1, -1, 2, -2):
+        pl.semaphore_signal(barrier, inc=1, device_id=dev(zmod(z + step), c, h), device_id_type=MESH)
+    pl.semaphore_signal(barrier, inc=1, device_id=sib, device_id_type=MESH)
+    pl.semaphore_signal(barrier, inc=1, device_id=extra, device_id_type=MESH)
+    for step in (1, 2, 3):
+        for hh in (hid_at(step, 0), hid_at(0, step)):
+            pl.semaphore_signal(barrier, inc=1, device_id=dev(z, c, hh), device_id_type=MESH)
+
     load_act = pltpu.make_async_copy(act_hbm, act.at[pl.ds(HALO, TOK), :], local_sem.at[0])
     own_rows = pl.ds(pl.multiple_of(s * 128, 128), 128)
     load_in = pltpu.make_async_copy(wi_hbm, w_in.at[own_rows, :], local_sem.at[1])
@@ -153,15 +162,6 @@
     load_gate.start()
     load_act.start()
 
-    barrier = pltpu.get_barrier_semaphore()
-    for step in (1, -1, 2, -2):
-        pl.semaphore_signal(barrier, inc=1, device_id=dev(zmod(z + step), c, h), device_id_type=MESH)
-    pl.semaphore_signal(barrier, inc=1, device_id=sib, device_id_type=MESH)
-    pl.semaphore_signal(barrier, inc=1, device_id=extra, device_id_type=MESH)
-    for step in (1, 2, 3):
-        for hh in (hid_at(step, 0), hid_at(0, step)):
-            pl.semaphore_signal(barrier, inc=1, device_id=dev(z, c, hh), device_id_type=MESH)
-
     for item in small:
         item.wait()
     tile = wgr_ref[...].astype(F32).T
@@ -357,9 +357,6 @@
     first(1)
     first(2)
     send_halo.start()
-    load_gate.wait()
-    first(3)
-    first(4)
     scaled = (wo_ref[...].astype(F32) * gain_ref[...]).astype(BF16)
 
     @pl.when(is_source)
@@ -393,6 +390,9 @@
 
     serve((0,), 1)
     serve(IN, 1)
+    load_gate.wait()
+    first(3)
+    first(4)
     load_act.wait()
     send_halo.wait()
     for kind in (0, 1):
@@ -492,10 +492,17 @@
     fresh1 = jnp.dot(bct[0:128, 256:512], weighted[256:512], preferred_element_type=F32)
     end_own = decay1 * fresh0 + fresh1
     total_own = decay0 * decay1
-    th, tl = split(jnp.broadcast_to(total_own, (8, 256)))
-    tail = jnp.concatenate([th.astype(F32), tl.astype(F32)], axis=0).astype(BF16)
+    def decay_rows(value):
+        high, low = split(jnp.broadcast_to(value, (8, value.shape[1])))
+        first_row = lax.broadcasted_iota(jnp.int32, (8, value.shape[1]), 0) == 0
+        return jnp.where(first_row, high.astype(F32), low.astype(F32)).astype(BF16)
+
+    def read_decay(rows):
+        rows = rows.astype(F32)
+        return rows[0:1] + rows[1:2]
+
     e_own[0:128, :] = end_own.astype(BF16)
-    e_own[128:144, :] = tail
+    e_own[128:136, :] = decay_rows(total_own)
     swap = remote(e_own, e_sib, es.at[0], es.at[1], sib)
     swap.start()
 
@@ -503,7 +510,7 @@
     swap.wait()
 
     end_sib = e_sib[0:128, :].astype(F32)
-    total_sib = e_sib[128:129, :].astype(F32) + e_sib[136:137, :].astype(F32)
+    total_sib = read_decay(e_sib[128:136, :])
 
     def my_half(value):
         return jnp.where(c == 0, value[:, 0:128], value[:, 128:256])
@@ -512,10 +519,8 @@
     chip_end = second_decay * jnp.where(c == 0, end_own, end_sib) + jnp.where(
         c == 0, end_sib, end_own
     )
-    chip_total = jnp.broadcast_to(my_half(total_own * total_sib), (8, 128))
-    th, tl = split(chip_total)
     tbuf[z, 0:128, :] = my_half(chip_end).astype(BF16)
-    tbuf[z, 128:144, :] = jnp.concatenate([th.astype(F32), tl.astype(F32)], axis=0).astype(BF16)
+    tbuf[z, 128:136, :] = decay_rows(my_half(total_own * total_sib))
 
     def t_send(d, k, hop):
         ref = tbuf.at[origin(d, k)]
@@ -595,7 +600,7 @@
     prefix = jnp.zeros((128, 128), F32)
     for k in range(15, 0, -1):
         zz = zmod(z - k)
-        decay = tbuf[zz, 128:129, :].astype(F32) + tbuf[zz, 136:137, :].astype(F32)
+        decay = read_decay(tbuf[zz, 128:136, :])
         joined = decay * prefix + tbuf[zz, 0:128, :].astype(F32)
         prefix = jnp.where(z >= k, joined, prefix)
     pbuf[...] = prefix
@@ -859,9 +864,9 @@
             pltpu.VMEM((256, TOK), BF16),
             pltpu.VMEM((TOK, 256), BF16),
             pltpu.VMEM((TOK, 128), F32),
-            pltpu.VMEM((144, 256), BF16),
-            pltpu.VMEM((144, 256), BF16),
-            pltpu.VMEM((16, 144, 128), BF16),
+            pltpu.VMEM((136, 256), BF16),
+            pltpu.VMEM((136, 256), BF16),
+            pltpu.VMEM((16, 136, 128), BF16),
             pltpu.VMEM((128, 128), F32),
             pltpu.VMEM((128, 128), F32),
             dma((3,)),

time: 98.5 us -> 98.2 us (level)
  no operation moved by 1% of the time
where the time goes in v6:
time: 98.2 us; the launch traced here: 98.1 us
  Pallas kernels  96.4 us (98%)
  local copies, waits for them, and re-layouts  1.67 us (2%)
    pallas_call x1, Pallas kernels, local(): pl.pallas_call(kernel, out_shape=jax.ShapeDtypeStruct((TOK, 256), BF16),...  96.4 us

profile of v6, /device:TPU:1, one launch (start us, length us, event | category | flops | bytes accessed | tf_op | source)
XLA Modules:
  0.0 98.1 jit_solution(6691668120482092260)
XLA Ops:
  0.0 96.4 %shard_map.118 = bf16[512,256]{1,0:T(8,128)(2,1)} custom-call(bf16[512,4096]{1,0:T(8,128)(2,1)} %act_hbm.1, bf16[128,256]{1,0:T(8,128)(2,1)} %wi_hbm.1, bf16[128,256]{1,0:T(8,128)(2,1)} %wg_hbm.1, bf16[128,256]{1,0:T(8,128)(2,1)} %wo_hbm.1, bf16[128,1024]{1,0:T(8,128)(2,1)} %wgr_hbm.1, bf16[64,128]{1,0:T(8,128)(2,1)} %bitcast.2, f32[4,256]{1,0:T(4,128)} %tapi_hbm.1, ...), custom_call_target="tpu_custom_call" | custom-call | tf_op jit(solution)/shard_map/pallas_call | solution.py:826
  96.4 1.7 %copy.14 = bf16[512,256]{1,0:T(8,128)(2,1)} copy(bf16[512,256]{1,0:T(8,128)(2,1)} %shard_map.118) | data formatting | bytes 524288
